TPU v7x, 128 devices: a whole 4x4x4 slice. The times are simulated.
128 devices in a mesh: row: 8 (over z, y_hi), col: 16 (over x, y_lo, core).
Axes of the slice: x: 4, y: 4 (y_hi: 2, y_lo: 2; y = y_hi * 2 + y_lo), z: 4, core: 2. Of those that a mesh axis runs over, the one named last changes fastest.
Arguments:
- tokens: bfloat16 [1536, 14336], P('col', 'row'), may hold values from -6 to 6
- weight_in: bfloat16 [14336, 14336], P('row', 'col'), may hold values from -0.046875 to 0.046875
- bias_hidden: float32 [14336], P('col'), may hold values from -3 to 3
- weight_out: bfloat16 [14336, 14336], P('col', 'row'), may hold values from -0.046875 to 0.046875
- out_grad: bfloat16 [1536, 14336], P('col', 'row'), may hold values from -0.75 to 0.75
Outputs:
- grad_tokens: bfloat16 [1536, 14336], P('col', 'row')
- grad_weight_in: float32 [14336, 14336], P('row', 'col')
- grad_bias: float32 [14336], P('col')
- grad_weight_out: float32 [14336, 14336], P('col', 'row')
All inputs are finite; a program needn't handle non-finite values.
Results may differ from a plain program's by a relative error of at most 0.007.
Values may be sent and summed in bfloat16 or wider, within the bound.
A program may use at most 128 MiB of HBM per device.

v0:
```python
import jax
import jax.numpy as jnp
from jax import lax
from jax.sharding import PartitionSpec as P

GELU_SCALE = 0.7978845608
GELU_CUBIC = 0.044715


def gelu_parts(values):
    inner = GELU_SCALE * (values + GELU_CUBIC * values * values * values)
    tangent = jnp.tanh(inner)
    result = 0.5 * values * (1.0 + tangent)
    slope = 0.5 * (1.0 + tangent) + 0.5 * values * (1.0 - tangent * tangent) * GELU_SCALE * (
        1.0 + 3.0 * GELU_CUBIC * values * values
    )
    return (result, slope)


def contract_rows(left, right):
    return lax.dot_general(
        left, right, (((0,), (0,)), ((), ())), preferred_element_type=jnp.float32
    )


def contract_cols(left, right):
    return lax.dot_general(
        left, right, (((1,), (1,)), ((), ())), preferred_element_type=jnp.float32
    )


def local(tokens, weight_in, bias_hidden, weight_out, out_grad):
    tok_all, grad_all = (
        lax.all_gather(tokens, "col", axis=0, tiled=True),
        lax.all_gather(out_grad, "col", axis=0, tiled=True),
    )
    pre_part = jnp.dot(tok_all, weight_in, preferred_element_type=jnp.float32)
    act_part = contract_cols(grad_all, weight_out)
    pre_mine, act_mine = (
        lax.psum_scatter(pre_part, "row", scatter_dimension=0, tiled=True),
        lax.psum_scatter(act_part, "row", scatter_dimension=0, tiled=True),
    )
    result, slope = gelu_parts(pre_mine + bias_hidden)
    act_local = result.astype(jnp.bfloat16)
    pre_grad_local = (act_mine * slope).astype(jnp.bfloat16)
    bias_local = jnp.sum(pre_grad_local, axis=0, dtype=jnp.float32)
    act_all, pre_grad_all = (
        lax.all_gather(act_local, "row", axis=0, tiled=True),
        lax.all_gather(pre_grad_local, "row", axis=0, tiled=True),
    )
    grad_bias = lax.psum(bias_local, "row")
    grad_weight_out = contract_rows(act_all, grad_all)
    grad_weight_in = contract_rows(tok_all, pre_grad_all)
    grad_tokens = lax.psum_scatter(
        contract_cols(pre_grad_all, weight_in), "col", scatter_dimension=0, tiled=True
    ).astype(jnp.bfloat16)
    return (grad_tokens, grad_weight_in, grad_bias, grad_weight_out)


def solution(mesh):
    placed = (P("col", "row"), P("row", "col"), P("col"), P("col", "row"), P("col", "row"))
    return jax.shard_map(
        local,
        mesh=mesh,
        in_specs=placed,
        out_specs=(P("col", "row"), P("row", "col"), P("col"), P("col", "row")),
        check_vma=False,
    )
```

profile of v0, /device:TPU:1, one launch (start us, length us, event | category | flops | bytes accessed | tf_op | source)
XLA Modules:
  0.0 540.9 jit_solution(17161725866408645790)
XLA Ops:
  7.2 0.0 copy-start
  7.2 0.0 all-gather.5.cloned.1.call-start
  7.2 0.7 all-gather.5.cloned.1.call-update
  7.9 0.0 all-gather.7.cloned.1.call-start
  8.0 0.7 all-gather.7.cloned.1.call-update
  8.7 0.0 reduce-scatter.4.cloned.1.call-start
  8.7 44.7 %all-gather.5.cloned.1.call-done = bf16[1536,1792]{1,0:T(8,128)(2,1)} async-done(((bf16[96,1792]{1,0:T(8,128)(2,1)}), bf16[1536,1792]{1,0:T(8,128)(2,1)}) %all-gather.5.cloned.1.call-update) | async-done | bytes 5505040 | tf_op jit(solution)/shard_map/all_gather | solution.py:35
  53.4 10.3 %fusion.8 = f32[1536,896]{1,0:T(8,128)} fusion(bf16[1536,1792]{1,0:T(8,128)(2,1)} %all-gather.5.cloned.1.call-done, bf16[896,1792]{1,0:T(8,128)(2,1)} %param.8), kind=kOutput, calls=%fused_computation.12 | convolution fusion | flops 4932501504 | bytes 14221312 | tf_op jit(solution)/shard_map/dot_general | solution.py:27
  63.8 0.0 reduce-scatter.4.cloned.1.call-update
  63.8 0.0 reduce-scatter.6.cloned.1.call-start
  63.8 31.1 %all-gather.7.cloned.1.call-done = bf16[1536,1792]{1,0:T(8,128)(2,1)} async-done(((bf16[96,1792]{1,0:T(8,128)(2,1)}), bf16[1536,1792]{1,0:T(8,128)(2,1)}) %all-gather.7.cloned.1.call-update) | async-done | bytes 5505040 | tf_op jit(solution)/shard_map/all_gather | solution.py:34
  94.9 0.0 copy-done
  94.9 9.3 %fusion.9 = f32[1536,896]{1,0:T(8,128)} fusion(bf16[1536,1792]{1,0:T(8,128)(2,1)} %all-gather.7.cloned.1.call-done, bf16[1792,896]{1,0:T(8,128)(2,1)S(1)} %copy-done), kind=kOutput, calls=%fused_computation.13 | convolution fusion | flops 4932501504 | bytes 14221312 | tf_op jit(solution)/shard_map/dot_general | solution.py:37
  104.2 0.0 copy-start.2
  104.3 0.0 reduce-scatter.6.cloned.1.call-update
  104.3 0.0 all-gather.9.cloned.1.call-start
  104.3 86.9 %reduce-scatter.4.cloned.1.call-done = f32[192,896]{1,0:T(8,128)} async-done(((f32[1536,896]{1,0:T(8,128)}), f32[192,896]{1,0:T(8,128)}) %reduce-scatter.4.cloned.1.call-update) | async-done | bytes 688144 | tf_op jit(solution)/shard_map/reduce_scatter | solution.py:41
  191.2 96.3 %reduce-scatter.6.cloned.1.call-done = f32[192,896]{1,0:T(8,128)} async-done(((f32[1536,896]{1,0:T(8,128)}), f32[192,896]{1,0:T(8,128)}) %reduce-scatter.6.cloned.1.call-update) | async-done | bytes 688144 | tf_op jit(solution)/shard_map/reduce_scatter | solution.py:40
  287.5 0.0 copy-done.2
  287.5 2.7 convert_reduce_fusion
  290.2 0.0 all-gather.9.cloned.1.call-update
  290.2 0.0 all-gather.11.cloned.1.call-start
  290.3 0.5 all-gather.11.cloned.1.call-update
  290.8 0.0 reduce-scatter.8.cloned.1.call-start
  290.8 57.9 %all-gather.9.cloned.1.call-done = bf16[1536,896]{1,0:T(8,128)(2,1)} async-done(((bf16[192,896]{1,0:T(8,128)(2,1)}), bf16[1536,896]{1,0:T(8,128)(2,1)}) %all-gather.9.cloned.1.call-update) | async-done | bytes 2752528 | tf_op jit(solution)/shard_map/all_gather | solution.py:49
  348.8 9.9 %fusion.10 = f32[1536,1792]{1,0:T(8,128)} fusion(bf16[1536,896]{1,0:T(8,128)(2,1)} %all-gather.9.cloned.1.call-done, bf16[1792,896]{1,0:T(8,128)(2,1)S(1)} %copy-done), kind=kOutput, calls=%fused_computation.14 | convolution fusion | flops 4932501504 | bytes 16973824 | tf_op jit(solution)/shard_map/dot_general | solution.py:27
  358.7 0.0 copy-start.3
  358.7 0.0 reduce-scatter.8.cloned.1.call-update
  358.7 17.6 %psum.7 = f32[896]{0:T(1024)} all-reduce(f32[896]{0:T(1024)S(1)} %get-tuple-element.8), channel_id=1, replica_groups=mesh['row'=8,'col'=16] {'row'}, use_global_device_ids=true, to_apply=%region_4.0 | all-reduce | flops 896 | bytes 7168 | tf_op jit(solution)/shard_map/psum | solution.py:51
  376.3 0.0 copy-done.3
  376.3 10.5 %convolution_bitcast_fusion = f32[1792,896]{0,1:T(8,128)} fusion(bf16[1536,896]{1,0:T(8,128)(2,1)S(1)} %copy-done.3, bf16[1536,1792]{1,0:T(8,128)(2,1)} %all-gather.7.cloned.1.call-done), kind=kOutput, calls=%fused_computation | convolution fusion | flops 4932501504 | bytes 14680064 | tf_op jit(solution)/shard_map/dot_general | solution.py:21
  386.8 0.0 copy-start.1
  386.8 8.0 %copy.9 = f32[1792,896]{1,0:T(8,128)} copy(f32[1792,896]{0,1:T(8,128)} %convolution_bitcast_fusion) | data formatting | bytes 12845056
  394.8 13.5 %all-gather.11.cloned.1.call-done = bf16[1536,896]{1,0:T(8,128)(2,1)} async-done(((bf16[192,896]{1,0:T(8,128)(2,1)}), bf16[1536,896]{1,0:T(8,128)(2,1)}) %all-gather.11.cloned.1.call-update) | async-done | bytes 2752528 | tf_op jit(solution)/shard_map/all_gather | solution.py:48
  408.3 11.4 %fusion.11 = f32[896,1792]{1,0:T(8,128)} fusion(bf16[1536,896]{1,0:T(8,128)(2,1)} %all-gather.11.cloned.1.call-done, bf16[1536,1792]{1,0:T(8,128)(2,1)} %all-gather.5.cloned.1.call-done), kind=kOutput, calls=%fused_computation.15 | convolution fusion | flops 4932501504 | bytes 14680064 | tf_op jit(solution)/shard_map/dot_general | solution.py:21
  419.7 112.5 %reduce-scatter.8.cloned.1.call-done = f32[96,1792]{1,0:T(8,128)} async-done(((f32[1536,1792]{1,0:T(8,128)}), f32[96,1792]{1,0:T(8,128)}) %reduce-scatter.8.cloned.1.call-update) | async-done | bytes 688144 | tf_op jit(solution)/shard_map/reduce_scatter | solution.py:54
  532.2 1.9 convert_element_type.13
  534.0 0.0 copy-done.1
Async XLA Ops:
  7.2 87.8 %copy-start = (bf16[1792,896]{1,0:T(8,128)(2,1)S(1)}, bf16[1792,896]{1,0:T(8,128)(2,1)}, u32[]{:S(2)}) copy-start(bf16[1792,896]{1,0:T(8,128)(2,1)} %param.6) | copy-start | bytes 9633796
  7.2 46.2 %all-gather.5.cloned.1.call-start = ((), (), s32[]{:S(2)}) async-start(), calls=%async_computation.3 | async-start | bytes 5849088 | tf_op jit(solution)/shard_map/all_gather | solution.py:35
  7.9 87.0 %all-gather.7.cloned.1.call-start = ((), (), s32[]{:S(2)}) async-start(), calls=%async_computation.5 | async-start | bytes 5849088 | tf_op jit(solution)/shard_map/all_gather | solution.py:34
  8.7 182.5 %reduce-scatter.4.cloned.1.call-start = ((), (), s32[]{:S(2)}) async-start(), calls=%async_computation.4 | async-start | bytes 6193152 | tf_op jit(solution)/shard_map/reduce_scatter | solution.py:41
  63.8 223.7 %reduce-scatter.6.cloned.1.call-start = ((), (), s32[]{:S(2)}) async-start(), calls=%async_computation.6 | async-start | bytes 6193152 | tf_op jit(solution)/shard_map/reduce_scatter | solution.py:40
  104.2 183.3 %copy-start.2 = (f32[896]{0:T(1024)S(1)}, f32[896]{0:T(1024)}, u32[]{:S(2)}) copy-start(f32[896]{0:T(1024)} %param.7) | copy-start | bytes 10756
  104.3 244.5 %all-gather.9.cloned.1.call-start = ((), (), s32[]{:S(2)}) async-start(), calls=%async_computation.7 | async-start | bytes 3096576 | tf_op jit(solution)/shard_map/all_gather | solution.py:49
  290.2 118.1 %all-gather.11.cloned.1.call-start = ((), (), s32[]{:S(2)}) async-start(), calls=%async_computation.9 | async-start | bytes 3096576 | tf_op jit(solution)/shard_map/all_gather | solution.py:48
  290.8 241.4 %reduce-scatter.8.cloned.1.call-start = ((), (), s32[]{:S(2)}) async-start(), calls=%async_computation.8 | async-start | bytes 11698176 | tf_op jit(solution)/shard_map/reduce_scatter | solution.py:54
  358.7 17.6 %copy-start.3 = (bf16[1536,896]{1,0:T(8,128)(2,1)S(1)}, bf16[1536,896]{1,0:T(8,128)(2,1)}, u32[]{:S(2)}) copy-start(bf16[1536,896]{1,0:T(8,128)(2,1)} %all-gather.9.cloned.1.call-done) | copy-start | bytes 8257540
  386.8 147.2 %copy-start.1 = (bf16[1792,896]{1,0:T(8,128)(2,1)S(1)}, bf16[1792,896]{1,0:T(8,128)(2,1)}, u32[]{:S(2)}) copy-start(bf16[1792,896]{1,0:T(8,128)(2,1)} %param.6) | copy-start | bytes 9633796
Sparse Core Ops, SparseCore 0:
  9.7 43.6 all-gather.4
  55.1 39.7 all-gather.6
  99.4 91.7 reduce-scatter.3
  196.0 91.4 reduce-scatter.5
  290.3 58.3 all-gather.8
  350.9 57.3 all-gather.10
  410.7 121.3 reduce-scatter.7
where the time goes:
time: 541 us
  waiting for transfers between devices  445 us (82%)
  matrix products  51.5 us (10%)
  blocking collectives  17.6 us (3%)
  between operations  14.1 us (3%)
  local copies, waits for them, and re-layouts  7.99 us (1%)
    reduce_scatter x1, waiting for transfers between devices, local(): lax.psum_scatter(contract_cols(pre_grad_all, weight_in), 'col', scatter_d...  112 us
    reduce_scatter x1, waiting for transfers between devices, local(): lax.psum_scatter(pre_part, 'row', scatter_dimension=0, tiled=True)  96.3 us
    reduce_scatter x1, waiting for transfers between devices, local(): lax.psum_scatter(act_part, 'row', scatter_dimension=0, tiled=True)  86.9 us
    all_gather x1, waiting for transfers between devices, local(): lax.all_gather(pre_grad_local, 'row', axis=0, tiled=True)  57.9 us
    all_gather x1, waiting for transfers between devices, local(): lax.all_gather(out_grad, 'col', axis=0, tiled=True)  44.7 us
    all_gather x1, waiting for transfers between devices, local(): lax.all_gather(tokens, 'col', axis=0, tiled=True)  31.1 us
    dot_general x2, matrix products, contract_rows(): lax.dot_general(left, right, (((0,), (0,)), ((), ())), preferred_element_...  21.9 us
    dot_general x2, matrix products, contract_cols(): lax.dot_general(left, right, (((1,), (1,)), ((), ())), preferred_element_...  20.2 us
  transfers between devices with their start and end apart: 7, of which 7 were waited for; matrix products, arithmetic and copies ran while one was open for 11% of the time, Pallas kernels for 0%

commit v1 on v0

v1 whole, which is shorter than its diff:
```python
import jax
import jax.numpy as jnp
from jax import lax
from jax.experimental import pallas as pl
from jax.experimental.pallas import tpu as pltpu
from jax.sharding import PartitionSpec as P

GELU_SCALE = 0.7978845608
GELU_CUBIC = 0.044715
MESH = pl.DeviceIdType.MESH
BF16 = jnp.bfloat16
F32 = jnp.float32

CHUNKS = ((0, 0), (1, 0), (3, 0), (2, 0), (2, 1), (1, 1), (3, 1), (0, 1))
SLOT = {where: at for at, where in enumerate(CHUNKS)}
N_CHUNKS = len(CHUNKS)
N_MESSAGES = 192


def gelu_parts(values):
    inner = GELU_SCALE * (values + GELU_CUBIC * values * values * values)
    tangent = jnp.tanh(inner)
    result = 0.5 * values * (1.0 + tangent)
    slope = 0.5 * (1.0 + tangent) + 0.5 * values * (1.0 - tangent * tangent) * GELU_SCALE * (
        1.0 + 3.0 * GELU_CUBIC * values * values
    )
    return (result, slope)


def dot_nn(left, right):
    return lax.dot_general(left, right, (((1,), (0,)), ((), ())), preferred_element_type=F32)


def dot_nt(left, right):
    return lax.dot_general(left, right, (((1,), (1,)), ((), ())), preferred_element_type=F32)


def dot_tn(left, right):
    return lax.dot_general(left, right, (((0,), (0,)), ((), ())), preferred_element_type=F32)


def tiles(total, size):
    return [(at, min(size, total - at)) for at in range(0, total, size)]


def exchange_kernel(
    tok_h, win_h, bias, wout_h, og_h,
    gt, tok_o, og_o, act_o, pg_o,
    win, wout, tok, og, act, pg, part, r1, r2, comb, summed, summed_in,
    g_out, g_in, keep, keep_in, x2_out, x2_in, x1_out, x1_in,
    send_sem, recv_sem, local_sem,
):
    own, dm = tok_h.shape
    ff = win.shape[1]
    piece = 2 * own // 4
    half = dm // 2
    row, col = lax.axis_index("row"), lax.axis_index("col")
    z, yh = row // 2, row % 2
    x, yl, core = col // 4, (col // 2) % 2, col % 2

    def device(z_, yh_, x_, yl_, core_):
        return (z_ * 2 + yh_, (x_ * 2 + yl_) * 2 + core_)

    to_sib = device(z, yh, x, yl, 1 - core)
    to_yl = device(z, yh, x, 1 - yl, core)
    to_yh = device(z, 1 - yh, x, yl, core)
    to_xp, to_xm = device(z, yh, (x + 1) % 4, yl, core), device(z, yh, (x + 3) % 4, yl, core)
    to_zp, to_zm = device((z + 1) % 4, yh, x, yl, core), device((z + 3) % 4, yh, x, yl, core)
    z1, z2, z3 = (z + 1) % 4, (z + 2) % 4, (z + 3) % 4

    def rows(at):
        return pl.ds(pl.multiple_of(at * piece, piece), piece)

    copies = []

    def send(src, dst, target):
        at = len(copies)
        copy = pltpu.make_async_remote_copy(
            src_ref=src, dst_ref=dst, send_sem=send_sem.at[at], recv_sem=recv_sem.at[at],
            device_id=target, device_id_type=MESH,
        )
        copy.start()
        copies.append(copy)
        return copy

    locals_ = []

    def local_copy(src, dst):
        copy = pltpu.make_async_copy(src, dst, local_sem.at[len(locals_)])
        copy.start()
        locals_.append(copy)
        return copy

    barrier = pltpu.get_barrier_semaphore()
    for target in (to_sib, to_yl, to_yh, to_xp, to_xm, to_zp, to_zm):
        pl.semaphore_signal(barrier, inc=1, device_id=target, device_id_type=MESH)

    mine, other = pl.ds(0, own), pl.ds(own, own)
    load_tok = local_copy(tok_h, tok.at[0, mine])
    load_win = local_copy(win_h, win)
    load_og = local_copy(og_h, og.at[0, mine])
    load_wout = local_copy(wout_h, wout)
    pl.semaphore_wait(barrier, 7)

    gather = {}
    pairs = ((0, tok_h, tok), (1, og_h, og))
    for a, src, buf in pairs:
        gather[a, 0, "s"] = send(src, buf.at[0, other], to_sib)
        gather[a, SLOT[0, 1]] = send(src, buf.at[SLOT[0, 1], mine], to_yl)
        gather[a, SLOT[3, 0]] = send(src, buf.at[SLOT[3, 0], mine], to_xp)
        gather[a, SLOT[1, 0]] = send(src, buf.at[SLOT[1, 0], mine], to_xm)

    def buf_of(a):
        return (tok, og)[a]

    def relay_to_sibling(a, k):
        gather[a, k].wait_recv()
        buf = buf_of(a)
        gather[a, k, "s"] = send(buf.at[k, mine], buf.at[k, other], to_sib)

    def relay_far(dy):
        far = SLOT[2, dy]
        gather[0, far] = send(tok.at[SLOT[3, dy], mine], tok.at[far, mine], to_xp)
        gather[1, far] = send(og.at[SLOT[1, dy], mine], og.at[far, mine], to_xm)

    def relay_pair(a):
        buf, k = buf_of(a), SLOT[0, 1]
        gather[a, SLOT[3, 1]] = send(buf.at[k, mine], buf.at[SLOT[3, 1], mine], to_xp)
        gather[a, SLOT[1, 1]] = send(buf.at[k, mine], buf.at[SLOT[1, 1], mine], to_xm)

    red = {}

    def partial_pre(k):
        gather[0, k, "s"].wait_recv()
        if k == 0:
            load_tok.wait()
            load_win.wait()
        for at, size in tiles(ff, 256):
            part[k, 0, :, at : at + size] = dot_nn(tok[k], win[:, at : at + size]).astype(BF16)
        red[k, "1p"] = send(part.at[k, 0, rows(z2)], r1.at[k, 0], to_zp)
        red[k, "2pm"] = send(part.at[k, 0, rows(z3)], r2.at[k, 1], to_zm)
        local_copy(tok.at[k], tok_o.at[k])

    def partial_act(k):
        gather[1, k, "s"].wait_recv()
        if k == 0:
            load_og.wait()
            load_wout.wait()
        for at, size in tiles(ff, 256):
            part[k, 1, :, at : at + size] = dot_nt(og[k], wout[at : at + size, :]).astype(BF16)
        red[k, "1a"] = send(part.at[k, 1, rows(z2)], r1.at[k, 1], to_zm)
        red[k, "2ap"] = send(part.at[k, 1, rows(z1)], r2.at[k, 2], to_zp)
        local_copy(og.at[k], og_o.at[k])

    def combine(k):
        red[k, "1p"].wait_recv()
        comb[k, 0] = (part[k, 0, rows(z1), :].astype(F32) + r1[k, 0].astype(F32)).astype(BF16)
        red[k, "2pp"] = send(comb.at[k, 0], r2.at[k, 0], to_zp)
        red[k, "1a"].wait_recv()
        comb[k, 1] = (part[k, 1, rows(z3), :].astype(F32) + r1[k, 1].astype(F32)).astype(BF16)
        red[k, "2am"] = send(comb.at[k, 1], r2.at[k, 3], to_zm)

    def reduce_pair(k):
        for name in ("2pm", "2ap", "2pp", "2am"):
            red[k, name].wait_recv()
        for a in range(2):
            total = part[k, a, rows(z), :].astype(F32) + (r2[k, 2 * a].astype(F32) + r2[k, 2 * a + 1].astype(F32))
            summed[k, a] = total.astype(BF16)
        red[k, "y"] = send(summed.at[k], summed_in.at[k], to_yh)

    def activate(k):
        red[k, "y"].wait_recv()
        pre = summed[k, 0].astype(F32) + summed_in[k, 0].astype(F32) + bias[...]
        act_grad = summed[k, 1].astype(F32) + summed_in[k, 1].astype(F32)
        result, slope = gelu_parts(pre)
        act[k, rows(z), :] = result.astype(BF16)
        pg[k, rows(z), :] = (act_grad * slope).astype(BF16)
        here = rows(z)
        red[k, "gpp"] = send(pg.at[k, here], pg.at[k, here], to_zp)
        red[k, "gpm"] = send(pg.at[k, here], pg.at[k, here], to_zm)
        red[k, "gap"] = send(act.at[k, here], act.at[k, here], to_zp)
        red[k, "gam"] = send(act.at[k, here], act.at[k, here], to_zm)

    def spread(k):
        red[k, "gpm"].wait_recv()
        red[k, "fp"] = send(pg.at[k, rows(z1)], pg.at[k, rows(z1)], to_zm)
        red[k, "gap"].wait_recv()
        red[k, "fa"] = send(act.at[k, rows(z3)], act.at[k, rows(z3)], to_zp)

    back = {}

    def grad_in(k):
        for name in ("gpp", "fp"):
            red[k, name].wait_recv()
        local_copy(pg.at[k], pg_o.at[k])
        for at, size in tiles(dm, 256):
            product = dot_nt(pg[k], win[at : at + size, :])
            keep[k, :, at : at + size] = product[:own].astype(BF16)
            g_out[k, :, at : at + size] = product[own:].astype(BF16)
        back[k, "s"] = send(g_out.at[k], g_in.at[k], to_sib)

    def store_act(k):
        for name in ("gam", "fa"):
            red[k, name].wait_recv()
        local_copy(act.at[k], act_o.at[k])

    def join_cores(k):
        back[k, "s"].wait_recv()
        dx, dy = CHUNKS[k]
        keep[k] = (keep[k].astype(F32) + g_in[k].astype(F32)).astype(BF16)
        if dy:
            back[dx, "y"] = send(keep.at[k], keep_in.at[dx], to_yl)

    def joined(dx, side):
        cols = pl.ds(side * half, half)
        return keep[SLOT[dx, 0], :, cols].astype(F32) + keep_in[dx, :, cols].astype(F32)

    def return_far():
        back[2, "y"].wait_recv()
        for side in range(2):
            x2_out[side] = joined(2, side).astype(BF16)
        back["far", 0] = send(x2_out.at[0], x2_in.at[0], to_xp)
        back["far", 1] = send(x2_out.at[1], x2_in.at[1], to_xm)

    def return_near(dx):
        way, target = (0, to_xp) if dx == 1 else (1, to_xm)
        back[dx, "y"].wait_recv()
        x1_out[way, 1 - way] = joined(dx, 1 - way).astype(BF16)
        back["near", way, 1 - way] = send(x1_out.at[way, 1 - way], x1_in.at[way, 1 - way], target)
        back["far", way].wait_recv()
        x1_out[way, way] = (joined(dx, way) + x2_in[way].astype(F32)).astype(BF16)
        back["near", way, way] = send(x1_out.at[way, way], x1_in.at[way, way], target)

    def finish():
        back[0, "y"].wait_recv()
        for side in range(2):
            for way in range(2):
                back["near", way, side].wait_recv()
            total = joined(0, side) + (x1_in[0, side].astype(F32) + x1_in[1, side].astype(F32))
            gt[:, side * half : (side + 1) * half] = total.astype(BF16)

    def relays_first():
        for a in range(2):
            for k in (SLOT[1, 0], SLOT[3, 0]):
                relay_to_sibling(a, k)
        relay_far(0)
        for a in range(2):
            relay_to_sibling(a, SLOT[0, 1])
            relay_pair(a)

    def relays_second():
        for a in range(2):
            relay_to_sibling(a, SLOT[2, 0])

    def relays_third():
        for a in range(2):
            for k in (SLOT[1, 1], SLOT[3, 1]):
                relay_to_sibling(a, k)
        relay_far(1)

    def relays_fourth():
        for a in range(2):
            relay_to_sibling(a, SLOT[2, 1])

    def at(stage, k):
        if 0 <= k < N_CHUNKS:
            stage(k)

    partial_pre(0)
    partial_act(0)
    combine(0)
    reduce_pair(0)
    relays_first()
    for t in range(1, N_CHUNKS + 7):
        if t == 1:
            activate(0)
        if t == 2:
            relays_second()
        if t == 3:
            relays_third()
        if t == 4:
            relays_fourth()
        if t > 1:
            at(combine, t - 1)
        at(partial_pre, t)
        at(partial_act, t)
        if t > 2:
            at(activate, t - 2)
        at(spread, t - 3)
        at(grad_in, t - 4)
        at(store_act, t - 4)
        at(join_cores, t - 5)
        if t - 6 == SLOT[2, 1]:
            return_far()
        if t - 6 == SLOT[1, 1]:
            return_near(1)
        if t - 6 == SLOT[3, 1]:
            return_near(3)
        if t > 1:
            at(reduce_pair, t - 1)
    finish()
    for copy in copies:
        copy.wait_send()
    for copy in locals_[4:]:
        copy.wait()


def exchange(tokens, weight_in, bias_hidden, weight_out, out_grad):
    own, dm = tokens.shape
    ff = weight_in.shape[1]
    chunk, piece, half = 2 * own, own // 2, dm // 2
    n = N_CHUNKS
    any_space = pl.BlockSpec(memory_space=pl.ANY)
    vmem = pl.BlockSpec(memory_space=pltpu.VMEM)
    flops = 3 * 2 * n * chunk * dm * ff
    return pl.pallas_call(
        exchange_kernel,
        out_shape=(
            jax.ShapeDtypeStruct((own, dm), BF16),
            jax.ShapeDtypeStruct((n, chunk, dm), BF16),
            jax.ShapeDtypeStruct((n, chunk, dm), BF16),
            jax.ShapeDtypeStruct((n, chunk, ff), BF16),
            jax.ShapeDtypeStruct((n, chunk, ff), BF16),
        ),
        in_specs=[any_space, any_space, vmem, any_space, any_space],
        out_specs=(vmem, any_space, any_space, any_space, any_space),
        scratch_shapes=[
            pltpu.VMEM((dm, ff), BF16),
            pltpu.VMEM((ff, dm), BF16),
            pltpu.VMEM((n, chunk, dm), BF16),
            pltpu.VMEM((n, chunk, dm), BF16),
            pltpu.VMEM((n, chunk, ff), BF16),
            pltpu.VMEM((n, chunk, ff), BF16),
            pltpu.VMEM((n, 2, chunk, ff), BF16),
            pltpu.VMEM((n, 2, piece, ff), BF16),
            pltpu.VMEM((n, 4, piece, ff), BF16),
            pltpu.VMEM((n, 2, piece, ff), BF16),
            pltpu.VMEM((n, 2, piece, ff), BF16),
            pltpu.VMEM((n, 2, piece, ff), BF16),
            pltpu.VMEM((n, own, dm), BF16),
            pltpu.VMEM((n, own, dm), BF16),
            pltpu.VMEM((n, own, dm), BF16),
            pltpu.VMEM((4, own, dm), BF16),
            pltpu.VMEM((2, own, half), BF16),
            pltpu.VMEM((2, own, half), BF16),
            pltpu.VMEM((2, 2, own, half), BF16),
            pltpu.VMEM((2, 2, own, half), BF16),
            pltpu.SemaphoreType.DMA((N_MESSAGES,)),
            pltpu.SemaphoreType.DMA((N_MESSAGES,)),
            pltpu.SemaphoreType.DMA((4 + 4 * n,)),
        ],
        compiler_params=pltpu.CompilerParams(
            collective_id=0, has_side_effects=True, vmem_limit_bytes=60 * 1024 * 1024
        ),
        cost_estimate=pl.CostEstimate(flops=flops, bytes_accessed=40_000_000, transcendentals=0),
        name="exchange",
    )(tokens, weight_in, bias_hidden.reshape(1, ff), weight_out, out_grad)


def local(tokens, weight_in, bias_hidden, weight_out, out_grad):
    grad_tokens, tok_all, grad_all, act_all, pre_grad_all = exchange(
        tokens, weight_in, bias_hidden, weight_out, out_grad
    )
    flat = lambda array: array.reshape(-1, array.shape[-1])
    tok_all, grad_all, act_all, pre_grad_all = map(flat, (tok_all, grad_all, act_all, pre_grad_all))
    grad_bias = jnp.sum(pre_grad_all, axis=0, dtype=F32)
    grad_weight_out = dot_tn(act_all, grad_all)
    grad_weight_in = dot_tn(tok_all, pre_grad_all)
    return (grad_tokens, grad_weight_in, grad_bias, grad_weight_out)


def solution(mesh):
    placed = (P("col", "row"), P("row", "col"), P("col"), P("col", "row"), P("col", "row"))
    return jax.shard_map(
        local,
        mesh=mesh,
        in_specs=placed,
        out_specs=(P("col", "row"), P("row", "col"), P("col"), P("col", "row")),
        check_vma=False,
    )
```

time: 541 us -> 172 us (0.32)
  waiting for transfers between devices: 445 us -> 0 us
  Pallas kernels: 0 us -> 146 us
  matrix products: 51.5 us -> 19.2 us
  blocking collectives: 17.6 us -> 0 us
  between operations: 14.1 us -> 0.67 us
  local copies, waits for them, and re-layouts: 7.99 us -> 2.01 us
    reduce_scatter x3 -> x0, waiting for transfers between devices: 296 us -> none  [the longest x1 112 us: local(): lax.psum_scatter(contract_cols(pre_grad_all, weight_in), 'col', scatter_d...]
    all_gather x4 -> x0, waiting for transfers between devices: 147 us -> none  [the longest x1 57.9 us: local(): lax.all_gather(pre_grad_local, 'row', axis=0, tiled=True)]
    pallas_call x0 -> x1, Pallas kernels: none -> 146 us  [exchange(): pl.pallas_call(exchange_kernel, out_shape=(jax.ShapeDtypeStruct((own, dm)...]
    dot_general x5 -> x2, matrix products: 51.5 us -> 19.2 us  [dot_tn(): lax.dot_general(left, right, (((0,), (0,)), ((), ())), preferred_element_...]
    psum x1 -> x0, blocking collectives: 17.6 us -> none  [local(): grad_bias = lax.psum(bias_local, 'row')]
    unnamed x9, local copies, waits for them, and re-layouts: 7.99 us -> 0.75 us
  transfers between devices with their start and end apart: 7 -> 0, of which waited for: 7 -> 0; matrix products, arithmetic and copies ran while one was open for 11% -> 0% of each run, Pallas kernels for 0% -> 0%
where the time goes in v1:
time: 172 us; the launch traced here: 169 us
  Pallas kernels  146 us (85%)
  matrix products  19.2 us (11%)
  local copies, waits for them, and re-layouts  2.01 us (1%)
    pallas_call x1, Pallas kernels, exchange(): pl.pallas_call(exchange_kernel, out_shape=(jax.ShapeDtypeStruct((own, dm)...  146 us
    dot_general x2, matrix products, dot_tn(): lax.dot_general(left, right, (((0,), (0,)), ((), ())), preferred_element_...  19.2 us

profile of v1, /device:TPU:1, one launch (start us, length us, event | category | flops | bytes accessed | tf_op | source)
XLA Modules:
  0.0 169.0 jit_solution(13565210738350337460)
XLA Ops:
  0.6 1.3 reshape.11.bias
  1.9 146.1 %exchange.1 = (bf16[96,1792]{1,0:T(8,128)(2,1)}, bf16[8,192,1792]{2,1,0:T(8,128)(2,1)}, bf16[8,192,1792]{2,1,0:T(8,128)(2,1)}, bf16[8,192,896]{2,1,0:T(8,128)(2,1)}, bf16[8,192,896]{2,1,0:T(8,128)(2,1)}) custom-call(bf16[96,1792]{1,0:T(8,128)(2,1)} %tok_h.1, bf16[1792,896]{1,0:T(8,128)(2,1)} %win_h.1, f32[1,896]{1,0:T(1,128)} %reshape.11.bias, ...), custom_call_target="tpu_custom_call" | custom-call | flops 14797504512 | bytes 40000000 | tf_op jit(solution)/shard_map/exchange/pallas_call | solution.py:316
  148.0 0.0 copy-start
  148.0 0.0 copy-start.2
  148.0 0.0 copy-start.3
  148.0 11.2 %convolution_bitcast_fusion.1 = f32[1792,896]{1,0:T(8,128)} fusion(bf16[8,192,1792]{2,1,0:T(8,128)(2,1)} %get-tuple-element.10, bf16[8,192,896]{2,1,0:T(8,128)(2,1)} %get-tuple-element.11), kind=kOutput, calls=%fused_computation.2 | convolution fusion | flops 4932501504 | bytes 14680064 | tf_op jit(solution)/shard_map/dot_general | solution.py:39
  159.3 0.0 copy-done
  159.3 1.1 convert_reduce_fusion
  160.3 0.0 copy-done.2
  160.3 0.0 copy-done.3
  160.3 0.0 copy-start.1
  160.3 8.0 %convolution_bitcast_fusion = f32[896,1792]{1,0:T(8,128)} fusion(bf16[8,192,896]{2,1,0:T(8,128)(2,1)S(1)} %copy-done.3, bf16[8,192,1792]{2,1,0:T(8,128)(2,1)S(1)} %copy-done.2), kind=kOutput, calls=%fused_computation.1 | convolution fusion | flops 4932501504 | bytes 14680064 | tf_op jit(solution)/shard_map/dot_general | solution.py:39
  168.3 0.0 copy-done.1
  168.3 0.7 copy.10
Async XLA Ops:
  148.0 11.3 %copy-start = (bf16[8,192,896]{2,1,0:T(8,128)(2,1)S(1)}, bf16[8,192,896]{2,1,0:T(8,128)(2,1)}, u32[]{:S(2)}) copy-start(bf16[8,192,896]{2,1,0:T(8,128)(2,1)} %get-tuple-element.11) | copy-start | bytes 8257540
  148.0 12.3 %copy-start.2 = (bf16[8,192,1792]{2,1,0:T(8,128)(2,1)S(1)}, bf16[8,192,1792]{2,1,0:T(8,128)(2,1)}, u32[]{:S(2)}) copy-start(bf16[8,192,1792]{2,1,0:T(8,128)(2,1)} %get-tuple-element.13) | copy-start | bytes 16515076
  148.0 12.3 %copy-start.3 = (bf16[8,192,896]{2,1,0:T(8,128)(2,1)S(1)}, bf16[8,192,896]{2,1,0:T(8,128)(2,1)}, u32[]{:S(2)}) copy-start(bf16[8,192,896]{2,1,0:T(8,128)(2,1)} %get-tuple-element.12) | copy-start | bytes 8257540
  160.3 8.0 %copy-start.1 = (bf16[96,1792]{1,0:T(8,128)(2,1)S(1)}, bf16[96,1792]{1,0:T(8,128)(2,1)}, u32[]{:S(2)}) copy-start(bf16[96,1792]{1,0:T(8,128)(2,1)} %get-tuple-element.18) | copy-start | bytes 1032196

commit v2 on v1

v2 whole, which is shorter than its diff:
```python
import jax
import jax.numpy as jnp
from jax import lax
from jax.experimental import pallas as pl
from jax.experimental.pallas import tpu as pltpu
from jax.sharding import PartitionSpec as P

GELU_SCALE = 0.7978845608
GELU_CUBIC = 0.044715
MESH = pl.DeviceIdType.MESH
BF16 = jnp.bfloat16
F32 = jnp.float32

CHUNKS = ((0, 0), (1, 0), (1, 1), (3, 0), (3, 1), (2, 0), (0, 1), (2, 1))
SCHEDULE = (
    ("start",), ("load",), ("pre", 0), ("actp", 0), ("combp", 0), ("comba", 0), ("rel", 0, 3), ("rel", 0, 1),
    ("rel", 0, 6), ("pre", 3), ("red", 0), ("pre", 1), ("combp", 3), ("rel", 1, 6), ("rel", 1, 3), ("rel", 1, 1),
    ("combp", 1), ("actp", 3), ("act", 0), ("actp", 1), ("rel", 0, 5), ("rel", 0, 2), ("comba", 3), ("sprp", 0),
    ("pre", 2), ("spra", 0), ("comba", 1), ("red", 3), ("rel", 1, 2), ("rel", 0, 4), ("combp", 2), ("grad", 0),
    ("actp", 2), ("pre", 4), ("store", 0), ("join", 0), ("red", 1), ("go", 0), ("rel", 1, 4), ("rel", 1, 5),
    ("comba", 2), ("act", 3), ("gi", 0), ("combp", 4), ("actp", 4), ("act", 1), ("red", 2), ("sprp", 3),
    ("spra", 3), ("rel", 0, 7), ("rel", 1, 7), ("pre", 7), ("comba", 4), ("actp", 7), ("sprp", 1), ("act", 2),
    ("pre", 5), ("actp", 5), ("spra", 1), ("grad", 3), ("store", 3), ("go", 3), ("combp", 7), ("join", 3),
    ("red", 4), ("near0", 1, 0), ("gi", 3), ("comba", 7), ("grad", 1), ("spra", 2), ("gi", 1), ("sprp", 2),
    ("act", 4), ("combp", 5), ("pre", 6), ("actp", 6), ("store", 1), ("join", 1), ("near0", 0, 0), ("go", 1),
    ("comba", 5), ("red", 7), ("store", 2), ("go", 2), ("grad", 2), ("sprp", 4), ("gi", 2), ("spra", 4),
    ("join", 2), ("near0", 0, 1), ("act", 7), ("combp", 6), ("comba", 6), ("red", 5), ("store", 4), ("go", 4),
    ("grad", 4), ("sprp", 7), ("gi", 4), ("spra", 7), ("join", 4), ("act", 5), ("near0", 1, 1), ("red", 6),
    ("grad", 7), ("store", 7), ("go", 7), ("sprp", 5), ("join", 7), ("gi", 7), ("spra", 5), ("act", 6), ("grad", 5),
    ("gi", 5), ("near1", 0, 1), ("sprp", 6), ("near1", 1, 1), ("store", 5), ("join", 5), ("go", 5), ("spra", 6),
    ("grad", 6), ("gi", 6), ("store", 6), ("join", 6), ("xred1",), ("go", 6), ("near1", 0, 0), ("near1", 1, 0),
    ("fin",),
)
SLOT = {where: at for at, where in enumerate(CHUNKS)}
N_CHUNKS = len(CHUNKS)
N_MESSAGES = 192


def gelu_parts(values):
    inner = GELU_SCALE * (values + GELU_CUBIC * values * values * values)
    tangent = jnp.tanh(inner)
    result = 0.5 * values * (1.0 + tangent)
    slope = 0.5 * (1.0 + tangent) + 0.5 * values * (1.0 - tangent * tangent) * GELU_SCALE * (
        1.0 + 3.0 * GELU_CUBIC * values * values
    )
    return (result, slope)


def dot_nn(left, right):
    return lax.dot_general(left, right, (((1,), (0,)), ((), ())), preferred_element_type=F32)


def dot_nt(left, right):
    return lax.dot_general(left, right, (((1,), (1,)), ((), ())), preferred_element_type=F32)


def dot_tn(left, right):
    return lax.dot_general(left, right, (((0,), (0,)), ((), ())), preferred_element_type=F32)


def tiles(total, size):
    return [(at, min(size, total - at)) for at in range(0, total, size)]


def exchange_kernel(
    tok_h, win_h, bias, wout_h, og_h,
    gt, gw_in, gw_out, grad_bias,
    win, wout, tok, og, act, pg, part, r1, r2, comb, summed, summed_in,
    g_out, g_in, keep, pair_out, pair_in, x2_out, x2_in, x1_out, x1_in, acc_in, acc_out,
    send_sem, recv_sem, local_sem,
):
    own, dm = tok_h.shape
    ff = win.shape[1]
    piece = 2 * own // 4
    half = dm // 2
    row, col = lax.axis_index("row"), lax.axis_index("col")
    z, yh = row // 2, row % 2
    x, yl, core = col // 4, (col // 2) % 2, col % 2

    def device(z_, yh_, x_, yl_, core_):
        return (z_ * 2 + yh_, (x_ * 2 + yl_) * 2 + core_)

    to_sib = device(z, yh, x, yl, 1 - core)
    to_yl = device(z, yh, x, 1 - yl, core)
    to_yh = device(z, 1 - yh, x, yl, core)
    to_xp, to_xm = device(z, yh, (x + 1) % 4, yl, core), device(z, yh, (x + 3) % 4, yl, core)
    to_zp, to_zm = device((z + 1) % 4, yh, x, yl, core), device((z + 3) % 4, yh, x, yl, core)
    z1, z2, z3 = (z + 1) % 4, (z + 2) % 4, (z + 3) % 4

    def rows(at):
        return pl.ds(pl.multiple_of(at * piece, piece), piece)

    copies = []

    def send(src, dst, target):
        at = len(copies)
        copy = pltpu.make_async_remote_copy(
            src_ref=src, dst_ref=dst, send_sem=send_sem.at[at], recv_sem=recv_sem.at[at],
            device_id=target, device_id_type=MESH,
        )
        copy.start()
        copies.append(copy)
        return copy

    locals_ = []

    def local_copy(src, dst):
        copy = pltpu.make_async_copy(src, dst, local_sem.at[len(locals_)])
        copy.start()
        locals_.append(copy)
        return copy

    barrier = pltpu.get_barrier_semaphore()
    for target in (to_sib, to_yl, to_yh, to_xp, to_xm, to_zp, to_zm):
        pl.semaphore_signal(barrier, inc=1, device_id=target, device_id_type=MESH)

    mine, other = pl.ds(0, own), pl.ds(own, own)
    sources = ((tok_h, tok.at[0, mine]), (win_h, win), (og_h, og.at[0, mine]), (wout_h, wout))
    loads = [local_copy(src, dst) for src, dst in sources]
    pl.semaphore_wait(barrier, 7)

    gather, red, back = {}, {}, {}
    bufs, halves = (tok, og), ((tok_h, tok), (og_h, og))

    def start():
        for a, (src, buf) in enumerate(halves):
            gather[a, 0, "s"] = send(src, buf.at[0, other], to_sib)
            for where, target in (((0, 1), to_yl), ((3, 0), to_xp), ((1, 0), to_xm)):
                k = SLOT[where]
                gather[a, k] = send(src, buf.at[k, mine], target)

    def load():
        for copy in loads:
            copy.wait()

    def relay(a, k):
        gather[a, k].wait_recv()
        buf, (dx, dy) = bufs[a], CHUNKS[k]
        onward = []
        if (dx, dy) == (0, 1):
            onward = [(SLOT[3, 1], to_xp), (SLOT[1, 1], to_xm)]
        elif (a, dx) == (0, 3):
            onward = [(SLOT[2, dy], to_xp)]
        elif (a, dx) == (1, 1):
            onward = [(SLOT[2, dy], to_xm)]
        for to, target in onward:
            gather[a, to] = send(buf.at[k, mine], buf.at[to, mine], target)
        gather[a, k, "s"] = send(buf.at[k, mine], buf.at[k, other], to_sib)

    def partial_pre(k):
        gather[0, k, "s"].wait_recv()
        for at, size in tiles(ff, 256):
            part[k, 0, :, at : at + size] = dot_nn(tok[k], win[:, at : at + size]).astype(BF16)
        red[k, "1p"] = send(part.at[k, 0, rows(z2)], r1.at[k, 0], to_zp)
        red[k, "2pm"] = send(part.at[k, 0, rows(z3)], r2.at[k, 1], to_zm)

    def partial_act(k):
        gather[1, k, "s"].wait_recv()
        for at, size in tiles(ff, 256):
            part[k, 1, :, at : at + size] = dot_nt(og[k], wout[at : at + size, :]).astype(BF16)
        red[k, "1a"] = send(part.at[k, 1, rows(z2)], r1.at[k, 1], to_zm)
        red[k, "2ap"] = send(part.at[k, 1, rows(z1)], r2.at[k, 2], to_zp)

    def combine(k, a, name, at, sent, into, target):
        red[k, name].wait_recv()
        comb[k, a] = (part[k, a, rows(at), :].astype(F32) + r1[k, a].astype(F32)).astype(BF16)
        red[k, sent] = send(comb.at[k, a], r2.at[k, into], target)

    def combine_pre(k):
        combine(k, 0, "1p", z1, "2pp", 0, to_zp)

    def combine_act(k):
        combine(k, 1, "1a", z3, "2am", 3, to_zm)

    def reduce_pair(k):
        for name in ("2pm", "2ap", "2pp", "2am"):
            red[k, name].wait_recv()
        for a in range(2):
            total = part[k, a, rows(z), :].astype(F32) + (r2[k, 2 * a].astype(F32) + r2[k, 2 * a + 1].astype(F32))
            summed[k, a] = total.astype(BF16)
        red[k, "y"] = send(summed.at[k], summed_in.at[k], to_yh)

    def activate(k):
        red[k, "y"].wait_recv()
        pre = summed[k, 0].astype(F32) + summed_in[k, 0].astype(F32) + bias[...].reshape(1, ff)
        act_grad = summed[k, 1].astype(F32) + summed_in[k, 1].astype(F32)
        result, slope = gelu_parts(pre)
        act[k, rows(z), :] = result.astype(BF16)
        pg[k, rows(z), :] = (act_grad * slope).astype(BF16)
        here = rows(z)
        red[k, "gpp"] = send(pg.at[k, here], pg.at[k, here], to_zp)
        red[k, "gpm"] = send(pg.at[k, here], pg.at[k, here], to_zm)
        red[k, "gap"] = send(act.at[k, here], act.at[k, here], to_zp)
        red[k, "gam"] = send(act.at[k, here], act.at[k, here], to_zm)

    def spread_pg(k):
        red[k, "gpm"].wait_recv()
        red[k, "fp"] = send(pg.at[k, rows(z1)], pg.at[k, rows(z1)], to_zm)

    def spread_act(k):
        red[k, "gap"].wait_recv()
        red[k, "fa"] = send(act.at[k, rows(z3)], act.at[k, rows(z3)], to_zp)

    def grad_in(k):
        for name in ("gpp", "fp"):
            red[k, name].wait_recv()
        for at, size in tiles(dm, 256):
            product = dot_nt(pg[k], win[at : at + size, :])
            keep[k, :, at : at + size] = product[:own].astype(BF16)
            g_out[k, :, at : at + size] = product[own:].astype(BF16)
        back[k, "s"] = send(g_out.at[k], g_in.at[k], to_sib)

    def store_act(k):
        for name in ("gam", "fa"):
            red[k, name].wait_recv()

    seen = set()

    def accumulate(acc, left, right, k, strip):
        first = id(acc) not in seen
        seen.add(id(acc))
        width = right.shape[-1]

        def body(i, carry):
            at = pl.ds(pl.multiple_of(i * strip, strip), strip)
            turned = left[k, :, at].T
            for to, size in tiles(width, 256):
                product = dot_nn(turned, right[k, :, to : to + size])
                acc[at, to : to + size] = product if first else acc[at, to : to + size] + product
            return carry

        lax.fori_loop(0, left.shape[-1] // strip, body, 0)

    def weight_out_part(k):
        accumulate(acc_out, act, og, k, 128)
        done["out"] += 1
        if done["out"] == N_CHUNKS:
            local_copy(acc_out, gw_out)

    def weight_in_part(k):
        accumulate(acc_in, tok, pg, k, 128)
        column = jnp.sum(pg[k].astype(F32), axis=0)
        grad_bias[...] = column if done["in"] == 0 else grad_bias[...] + column
        done["in"] += 1
        if done["in"] == N_CHUNKS:
            local_copy(acc_in, gw_in)

    done = {"out": 0, "in": 0}
    ways = ((1, to_xp), (3, to_xm))

    def cols(side):
        return pl.ds(side * half, half)

    def join_cores(k):
        back[k, "s"].wait_recv()
        dx, dy = CHUNKS[k]
        total = (keep[k].astype(F32) + g_in[k].astype(F32)).astype(BF16)
        if dx == 2:
            for side, (_, target) in enumerate(ways):
                x2_out[dy, side] = total[:, side * half : (side + 1) * half]
                back["far", side, dy] = send(x2_out.at[dy, side], x2_in.at[dy, side], target)
        else:
            keep[k] = total

    def return_near(way, dy):
        dx, target = ways[way]
        x1_out[dy, way, 1 - way] = keep[SLOT[dx, dy], :, cols(1 - way)]
        back["near", way, 1 - way, dy] = send(x1_out.at[dy, way, 1 - way], x1_in.at[dy, way, 1 - way], target)

    def return_both(way, dy):
        dx, target = ways[way]
        back["far", way, dy].wait_recv()
        own_part = keep[SLOT[dx, dy], :, cols(way)].astype(F32)
        x1_out[dy, way, way] = (own_part + x2_in[dy, way].astype(F32)).astype(BF16)
        back["near", way, way, dy] = send(x1_out.at[dy, way, way], x1_in.at[dy, way, way], target)

    def from_row(dy, side):
        for way in range(2):
            back["near", way, side, dy].wait_recv()
        both = x1_in[dy, 0, side].astype(F32) + x1_in[dy, 1, side].astype(F32)
        return keep[SLOT[0, dy], :, cols(side)].astype(F32) + both

    def pass_pair():
        for side in range(2):
            pair_out[:, cols(side)] = from_row(1, side).astype(BF16)
        back["y"] = send(pair_out, pair_in, to_yl)

    def finish():
        back["y"].wait_recv()
        for side in range(2):
            total = from_row(0, side) + pair_in[:, cols(side)].astype(F32)
            gt[:, side * half : (side + 1) * half] = total.astype(BF16)

    stages = {
        "start": start, "load": load, "rel": relay, "pre": partial_pre, "actp": partial_act,
        "combp": combine_pre, "comba": combine_act, "red": reduce_pair, "act": activate,
        "sprp": spread_pg, "spra": spread_act, "grad": grad_in, "store": store_act, "join": join_cores,
        "near0": return_near, "near1": return_both, "xred1": pass_pair, "fin": finish,
        "go": weight_out_part, "gi": weight_in_part,
    }
    for stage, *where in SCHEDULE:
        stages[stage](*where)
    for copy in copies:
        copy.wait_send()
    for copy in locals_[len(loads) :]:
        copy.wait()


def exchange(tokens, weight_in, bias_hidden, weight_out, out_grad):
    own, dm = tokens.shape
    ff = weight_in.shape[1]
    chunk, piece, half = 2 * own, own // 2, dm // 2
    n = N_CHUNKS
    any_space = pl.BlockSpec(memory_space=pl.ANY)
    vmem = pl.BlockSpec(memory_space=pltpu.VMEM)
    flops = 5 * 2 * n * chunk * dm * ff
    return pl.pallas_call(
        exchange_kernel,
        out_shape=(
            jax.ShapeDtypeStruct((own, dm), BF16),
            jax.ShapeDtypeStruct((dm, ff), F32),
            jax.ShapeDtypeStruct((ff, dm), F32),
            jax.ShapeDtypeStruct((ff,), F32),
        ),
        in_specs=[any_space, any_space, vmem, any_space, any_space],
        out_specs=(vmem, any_space, any_space, vmem),
        scratch_shapes=[
            pltpu.VMEM((dm, ff), BF16),
            pltpu.VMEM((ff, dm), BF16),
            pltpu.VMEM((n, chunk, dm), BF16),
            pltpu.VMEM((n, chunk, dm), BF16),
            pltpu.VMEM((n, chunk, ff), BF16),
            pltpu.VMEM((n, chunk, ff), BF16),
            pltpu.VMEM((n, 2, chunk, ff), BF16),
            pltpu.VMEM((n, 2, piece, ff), BF16),
            pltpu.VMEM((n, 4, piece, ff), BF16),
            pltpu.VMEM((n, 2, piece, ff), BF16),
            pltpu.VMEM((n, 2, piece, ff), BF16),
            pltpu.VMEM((n, 2, piece, ff), BF16),
            pltpu.VMEM((n, own, dm), BF16),
            pltpu.VMEM((n, own, dm), BF16),
            pltpu.VMEM((n, own, dm), BF16),
            pltpu.VMEM((own, dm), BF16),
            pltpu.VMEM((own, dm), BF16),
            pltpu.VMEM((2, 2, own, half), BF16),
            pltpu.VMEM((2, 2, own, half), BF16),
            pltpu.VMEM((2, 2, 2, own, half), BF16),
            pltpu.VMEM((2, 2, 2, own, half), BF16),
            pltpu.VMEM((dm, ff), F32),
            pltpu.VMEM((ff, dm), F32),
            pltpu.SemaphoreType.DMA((N_MESSAGES,)),
            pltpu.SemaphoreType.DMA((N_MESSAGES,)),
            pltpu.SemaphoreType.DMA((16,)),
        ],
        compiler_params=pltpu.CompilerParams(
            collective_id=0, has_side_effects=True, vmem_limit_bytes=63 * 1024 * 1024
        ),
        cost_estimate=pl.CostEstimate(flops=flops, bytes_accessed=40_000_000, transcendentals=0),
        name="exchange",
    )(tokens, weight_in, bias_hidden, weight_out, out_grad)


def local(tokens, weight_in, bias_hidden, weight_out, out_grad):
    grad_tokens, grad_weight_in, grad_weight_out, grad_bias = exchange(
        tokens, weight_in, bias_hidden, weight_out, out_grad
    )
    return (grad_tokens, grad_weight_in, grad_bias, grad_weight_out)


def solution(mesh):
    placed = (P("col", "row"), P("row", "col"), P("col"), P("col", "row"), P("col", "row"))
    return jax.shard_map(
        local,
        mesh=mesh,
        in_specs=placed,
        out_specs=(P("col", "row"), P("row", "col"), P("col"), P("col", "row")),
        check_vma=False,
    )
```

time: 172 us -> 147 us (0.85)
  matrix products: 19.2 us -> 0 us
  Pallas kernels: 146 us -> 133 us
  local copies, waits for them, and re-layouts: 2.01 us -> 11.4 us
    dot_general x2 -> x0, matrix products: 19.2 us -> none  [dot_tn(): lax.dot_general(left, right, (((0,), (0,)), ((), ())), preferred_element_...]
    pallas_call x1, Pallas kernels: 146 us -> 133 us  [exchange(): pl.pallas_call(exchange_kernel, out_shape=(jax.ShapeDtypeStruct((own, dm)...]
    unnamed x9 -> x10, local copies, waits for them, and re-layouts: 0.75 us -> 11.4 us
where the time goes in v2:
time: 147 us; the launch traced here: 145 us
  Pallas kernels  133 us (90%)
  local copies, waits for them, and re-layouts  11.4 us (8%)
    pallas_call x1, Pallas kernels, exchange(): pl.pallas_call(exchange_kernel, out_shape=(jax.ShapeDtypeStruct((own, dm)...  133 us
    unnamed x10, local copies, waits for them, and re-layouts  11.4 us

profile of v2, /device:TPU:1, one launch (start us, length us, event | category | flops | bytes accessed | tf_op | source)
XLA Modules:
  0.0 144.7 jit_solution(3930991737590479169)
XLA Ops:
  0.6 132.7 %exchange.1 = (bf16[96,1792]{1,0:T(8,128)(2,1)}, f32[1792,896]{1,0:T(8,128)}, f32[896,1792]{1,0:T(8,128)}, f32[896]{0:T(1024)}) custom-call(bf16[96,1792]{1,0:T(8,128)(2,1)} %tok_h.1, bf16[1792,896]{1,0:T(8,128)(2,1)} %win_h.1, f32[896]{0:T(1024)} %bias.1, bf16[896,1792]{1,0:T(8,128)(2,1)} %wout_h.1, bf16[96,1792]{1,0:T(8,128)(2,1)} %og_h.1), custom_call_target="tpu_custom_call" | custom-call | flops 24662507520 | bytes 40000000 | tf_op jit(solution)/shard_map/exchange/pallas_call | solution.py:317
  133.4 0.0 slice-start
  133.4 1.9 %copy.13 = bf16[96,1792]{1,0:T(8,128)(2,1)} copy(bf16[96,1792]{1,0:T(8,128)(2,1)} %get-tuple-element.16) | data formatting | bytes 688128
  135.2 0.0 copy-start
  135.2 0.0 slice-start.1
  135.3 6.1 %copy.14 = f32[1792,896]{1,0:T(8,128)} copy(f32[1792,896]{1,0:T(8,128)} %get-tuple-element.17) | data formatting | bytes 12845056
  141.4 0.0 copy-done
  141.4 0.6 copy.15
  142.0 0.0 slice-done
  142.0 0.0 slice-done.1
  142.0 2.7 %copy.16 = f32[896,1792]{1,0:T(8,128)} copy(f32[896,1792]{1,0:T(8,128)S(1)} %bitcast.1) | data formatting | bytes 12845056
  (1 shorter events, 0.0 us)
Async XLA Ops:
  133.4 8.6 %slice-start = ((s8[6422528]{0:T(1024)(128)(4,1)}), s8[4194304]{0:T(1024)(128)(4,1)S(1)}, s32[]{:S(2)}) async-start(s8[6422528]{0:T(1024)(128)(4,1)} %bitcast), calls=%async_computation | async-start | bytes 8388608
  135.2 6.1 %copy-start = (f32[896]{0:T(1024)S(1)}, f32[896]{0:T(1024)}, u32[]{:S(2)}) copy-start(f32[896]{0:T(1024)} %get-tuple-element.18) | copy-start | bytes 10756
  135.2 6.7 %slice-start.1 = ((s8[6422528]{0:T(1024)(128)(4,1)}), s8[2228224]{0:T(1024)(128)(4,1)S(1)}, s32[]{:S(2)}) async-start(s8[6422528]{0:T(1024)(128)(4,1)} %bitcast), calls=%async_computation.1 | async-start | bytes 4456448

commit v3 on v2

--- a/solution.py
+++ b/solution.py
@@ -1,3 +1,5 @@
+import functools
+
 import jax
 import jax.numpy as jnp
 from jax import lax
@@ -11,28 +13,34 @@
 BF16 = jnp.bfloat16
 F32 = jnp.float32
 
-CHUNKS = ((0, 0), (1, 0), (1, 1), (3, 0), (3, 1), (2, 0), (0, 1), (2, 1))
+CHUNKS = ((0, 0), (3, 0), (1, 0), (1, 1), (2, 0), (2, 1), (3, 1), (0, 1))
 SCHEDULE = (
-    ("start",), ("load",), ("pre", 0), ("actp", 0), ("combp", 0), ("comba", 0), ("rel", 0, 3), ("rel", 0, 1),
-    ("rel", 0, 6), ("pre", 3), ("red", 0), ("pre", 1), ("combp", 3), ("rel", 1, 6), ("rel", 1, 3), ("rel", 1, 1),
-    ("combp", 1), ("actp", 3), ("act", 0), ("actp", 1), ("rel", 0, 5), ("rel", 0, 2), ("comba", 3), ("sprp", 0),
-    ("pre", 2), ("spra", 0), ("comba", 1), ("red", 3), ("rel", 1, 2), ("rel", 0, 4), ("combp", 2), ("grad", 0),
-    ("actp", 2), ("pre", 4), ("store", 0), ("join", 0), ("red", 1), ("go", 0), ("rel", 1, 4), ("rel", 1, 5),
-    ("comba", 2), ("act", 3), ("gi", 0), ("combp", 4), ("actp", 4), ("act", 1), ("red", 2), ("sprp", 3),
-    ("spra", 3), ("rel", 0, 7), ("rel", 1, 7), ("pre", 7), ("comba", 4), ("actp", 7), ("sprp", 1), ("act", 2),
-    ("pre", 5), ("actp", 5), ("spra", 1), ("grad", 3), ("store", 3), ("go", 3), ("combp", 7), ("join", 3),
-    ("red", 4), ("near0", 1, 0), ("gi", 3), ("comba", 7), ("grad", 1), ("spra", 2), ("gi", 1), ("sprp", 2),
-    ("act", 4), ("combp", 5), ("pre", 6), ("actp", 6), ("store", 1), ("join", 1), ("near0", 0, 0), ("go", 1),
-    ("comba", 5), ("red", 7), ("store", 2), ("go", 2), ("grad", 2), ("sprp", 4), ("gi", 2), ("spra", 4),
-    ("join", 2), ("near0", 0, 1), ("act", 7), ("combp", 6), ("comba", 6), ("red", 5), ("store", 4), ("go", 4),
-    ("grad", 4), ("sprp", 7), ("gi", 4), ("spra", 7), ("join", 4), ("act", 5), ("near0", 1, 1), ("red", 6),
-    ("grad", 7), ("store", 7), ("go", 7), ("sprp", 5), ("join", 7), ("gi", 7), ("spra", 5), ("act", 6), ("grad", 5),
-    ("gi", 5), ("near1", 0, 1), ("sprp", 6), ("near1", 1, 1), ("store", 5), ("join", 5), ("go", 5), ("spra", 6),
-    ("grad", 6), ("gi", 6), ("store", 6), ("join", 6), ("xred1",), ("go", 6), ("near1", 0, 0), ("near1", 1, 0),
-    ("fin",),
+    ("start",), ("load",), ("pre", 0), ("actp", 0), ("combp", 0), ("comba", 0), ("rel", 0, 1), ("rel", 0, 2),
+    ("rel", 0, 7), ("pre", 1), ("red", 0), ("combp", 1), ("pre", 2), ("rel", 1, 1), ("rel", 1, 2), ("rel", 1, 7),
+    ("actp", 1), ("act", 0), ("actp", 2), ("combp", 2), ("rel", 0, 4), ("rel", 0, 3), ("comba", 1), ("sprp", 0),
+    ("pre", 3), ("spra", 0), ("comba", 2), ("red", 1), ("rel", 1, 4), ("rel", 0, 6), ("grad", 0), ("combp", 3),
+    ("pre", 4), ("actp", 4), ("store", 0), ("join", 0), ("red", 2), ("gb", 0), ("act", 1), ("rel", 1, 6),
+    ("rel", 1, 3), ("combp", 4), ("comba", 4), ("actp", 3), ("sprp", 1), ("act", 2), ("spra", 1), ("rel", 0, 5),
+    ("red", 4), ("comba", 3), ("pre", 5), ("rel", 1, 5), ("grad", 1), ("gb", 1), ("actp", 5), ("spra", 2),
+    ("sprp", 2), ("join", 1), ("near0", 1, 0), ("act", 4), ("store", 1), ("red", 3), ("combp", 5), ("pre", 6),
+    ("actp", 6), ("comba", 5), ("store", 2), ("grad", 2), ("act", 3), ("gb", 2), ("sprp", 4), ("spra", 4),
+    ("join", 2), ("near0", 0, 0), ("combp", 6), ("pre", 7), ("comba", 6), ("actp", 7), ("red", 5), ("sprp", 3),
+    ("spra", 3), ("store", 4), ("grad", 4), ("act", 5), ("gb", 4), ("combp", 7), ("join", 4), ("red", 6),
+    ("comba", 7), ("store", 3), ("go", 0, 3), ("grad", 3), ("go", 1, 3), ("sprp", 5), ("near1", 0, 0), ("act", 6),
+    ("spra", 5), ("near1", 1, 0), ("join", 3), ("near0", 0, 1), ("go", 2, 3), ("red", 7), ("gi", 0, 3),
+    ("gi", 1, 3), ("grad", 5), ("spra", 6), ("sprp", 6), ("gi", 2, 3), ("fin",), ("gi", 3, 3), ("store", 5),
+    ("join", 5), ("act", 7), ("grad", 6), ("store", 6), ("gb", 3), ("go", 0, 5), ("go", 1, 5), ("join", 6),
+    ("near0", 1, 1), ("sprp", 7), ("go", 2, 5), ("gi", 0, 5), ("spra", 7), ("near1", 0, 1), ("near1", 1, 1),
+    ("gi", 1, 5), ("gi", 2, 5), ("grad", 7), ("gi", 3, 5), ("store", 7), ("gb", 5), ("gb", 6), ("gb", 7),
+    ("join", 7), ("xred1",),
 )
 SLOT = {where: at for at, where in enumerate(CHUNKS)}
 N_CHUNKS = len(CHUNKS)
+GROUPS = {3: (0, 4), 5: (4, 6)}
+LATE = 6
+STRIP = 128
+OUT_STRIPS = ((0, 2), (2, 4), (4, 7))
+IN_STRIPS = ((0, 3), (3, 7), (7, 10), (10, 14))
 N_MESSAGES = 192
 
 
@@ -64,9 +72,9 @@
 
 def exchange_kernel(
     tok_h, win_h, bias, wout_h, og_h,
-    gt, gw_in, gw_out, grad_bias,
+    near_sum, pair_out, gw_in, gw_out, grad_bias, act_late, og_late, tok_late, pg_late,
     win, wout, tok, og, act, pg, part, r1, r2, comb, summed, summed_in,
-    g_out, g_in, keep, pair_out, pair_in, x2_out, x2_in, x1_out, x1_in, acc_in, acc_out,
+    g_out, g_in, keep, x2_out, x2_in, x1_out, x1_in, acc_in, acc_out,
     send_sem, recv_sem, local_sem,
 ):
     own, dm = tok_h.shape
@@ -89,6 +97,9 @@
 
     def rows(at):
         return pl.ds(pl.multiple_of(at * piece, piece), piece)
+
+    def late_rows(k):
+        return pl.ds((k - LATE) * 2 * own, 2 * own)
 
     copies = []
 
@@ -153,6 +164,8 @@
             part[k, 0, :, at : at + size] = dot_nn(tok[k], win[:, at : at + size]).astype(BF16)
         red[k, "1p"] = send(part.at[k, 0, rows(z2)], r1.at[k, 0], to_zp)
         red[k, "2pm"] = send(part.at[k, 0, rows(z3)], r2.at[k, 1], to_zm)
+        if k >= LATE:
+            local_copy(tok.at[k], tok_late.at[late_rows(k)])
 
     def partial_act(k):
         gather[1, k, "s"].wait_recv()
@@ -160,6 +173,8 @@
             part[k, 1, :, at : at + size] = dot_nt(og[k], wout[at : at + size, :]).astype(BF16)
         red[k, "1a"] = send(part.at[k, 1, rows(z2)], r1.at[k, 1], to_zm)
         red[k, "2ap"] = send(part.at[k, 1, rows(z1)], r2.at[k, 2], to_zp)
+        if k >= LATE:
+            local_copy(og.at[k], og_late.at[late_rows(k)])
 
     def combine(k, a, name, at, sent, into, target):
         red[k, name].wait_recv()
@@ -204,6 +219,8 @@
     def grad_in(k):
         for name in ("gpp", "fp"):
             red[k, name].wait_recv()
+        if k >= LATE:
+            local_copy(pg.at[k], pg_late.at[late_rows(k)])
         for at, size in tiles(dm, 256):
             product = dot_nt(pg[k], win[at : at + size, :])
             keep[k, :, at : at + size] = product[:own].astype(BF16)
@@ -213,39 +230,44 @@
     def store_act(k):
         for name in ("gam", "fa"):
             red[k, name].wait_recv()
-
-    seen = set()
-
-    def accumulate(acc, left, right, k, strip):
-        first = id(acc) not in seen
-        seen.add(id(acc))
-        width = right.shape[-1]
+        if k >= LATE:
+            local_copy(act.at[k], act_late.at[late_rows(k)])
+
+    started, done = set(), {"in": 0, "out": 0, "bias": 0}
+
+    def accumulate(acc, left, right, k, strips):
+        first = (id(acc), strips) not in started
+        started.add((id(acc), strips))
+        group = pl.ds(GROUPS[k][0], GROUPS[k][1] - GROUPS[k][0])
+        depth = (GROUPS[k][1] - GROUPS[k][0]) * 2 * own
 
         def body(i, carry):
-            at = pl.ds(pl.multiple_of(i * strip, strip), strip)
-            turned = left[k, :, at].T
-            for to, size in tiles(width, 256):
-                product = dot_nn(turned, right[k, :, to : to + size])
+            at = pl.ds(pl.multiple_of(i * STRIP, STRIP), STRIP)
+            turned = left[group, :, at].reshape(depth, STRIP).T
+            for to, size in tiles(right.shape[-1], 256):
+                product = dot_nn(turned, right[group, :, to : to + size].reshape(depth, size))
                 acc[at, to : to + size] = product if first else acc[at, to : to + size] + product
             return carry
 
-        lax.fori_loop(0, left.shape[-1] // strip, body, 0)
-
-    def weight_out_part(k):
-        accumulate(acc_out, act, og, k, 128)
+        lax.fori_loop(*strips, body, 0)
+
+    def weight_out_part(at, k):
+        accumulate(acc_out, act, og, k, OUT_STRIPS[at])
         done["out"] += 1
-        if done["out"] == N_CHUNKS:
+        if done["out"] == len(GROUPS) * len(OUT_STRIPS):
             local_copy(acc_out, gw_out)
 
-    def weight_in_part(k):
-        accumulate(acc_in, tok, pg, k, 128)
+    def weight_in_part(at, k):
+        accumulate(acc_in, tok, pg, k, IN_STRIPS[at])
+        done["in"] += 1
+        if done["in"] == len(GROUPS) * len(IN_STRIPS):
+            local_copy(acc_in, gw_in)
+
+    def bias_part(k):
         column = jnp.sum(pg[k].astype(F32), axis=0)
-        grad_bias[...] = column if done["in"] == 0 else grad_bias[...] + column
-        done["in"] += 1
-        if done["in"] == N_CHUNKS:
-            local_copy(acc_in, gw_in)
-
-    done = {"out": 0, "in": 0}
+        grad_bias[...] = grad_bias[...] + column if done["bias"] else column
+        done["bias"] += 1
+
     ways = ((1, to_xp), (3, to_xm))
 
     def cols(side):
@@ -283,20 +305,17 @@
     def pass_pair():
         for side in range(2):
             pair_out[:, cols(side)] = from_row(1, side).astype(BF16)
-        back["y"] = send(pair_out, pair_in, to_yl)
 
     def finish():
-        back["y"].wait_recv()
         for side in range(2):
-            total = from_row(0, side) + pair_in[:, cols(side)].astype(F32)
-            gt[:, side * half : (side + 1) * half] = total.astype(BF16)
+            near_sum[:, cols(side)] = from_row(0, side)
 
     stages = {
         "start": start, "load": load, "rel": relay, "pre": partial_pre, "actp": partial_act,
         "combp": combine_pre, "comba": combine_act, "red": reduce_pair, "act": activate,
         "sprp": spread_pg, "spra": spread_act, "grad": grad_in, "store": store_act, "join": join_cores,
         "near0": return_near, "near1": return_both, "xred1": pass_pair, "fin": finish,
-        "go": weight_out_part, "gi": weight_in_part,
+        "go": weight_out_part, "gi": weight_in_part, "gb": bias_part,
     }
     for stage, *where in SCHEDULE:
         stages[stage](*where)
@@ -311,19 +330,25 @@
     ff = weight_in.shape[1]
     chunk, piece, half = 2 * own, own // 2, dm // 2
     n = N_CHUNKS
+    late = (n - LATE) * chunk
     any_space = pl.BlockSpec(memory_space=pl.ANY)
     vmem = pl.BlockSpec(memory_space=pltpu.VMEM)
     flops = 5 * 2 * n * chunk * dm * ff
     return pl.pallas_call(
         exchange_kernel,
         out_shape=(
+            jax.ShapeDtypeStruct((own, dm), F32),
             jax.ShapeDtypeStruct((own, dm), BF16),
             jax.ShapeDtypeStruct((dm, ff), F32),
             jax.ShapeDtypeStruct((ff, dm), F32),
             jax.ShapeDtypeStruct((ff,), F32),
+            jax.ShapeDtypeStruct((late, ff), BF16),
+            jax.ShapeDtypeStruct((late, dm), BF16),
+            jax.ShapeDtypeStruct((late, dm), BF16),
+            jax.ShapeDtypeStruct((late, ff), BF16),
         ),
         in_specs=[any_space, any_space, vmem, any_space, any_space],
-        out_specs=(vmem, any_space, any_space, vmem),
+        out_specs=(vmem, vmem, any_space, any_space, vmem, *[any_space] * 4),
         scratch_shapes=[
             pltpu.VMEM((dm, ff), BF16),
             pltpu.VMEM((ff, dm), BF16),
@@ -340,8 +365,6 @@
             pltpu.VMEM((n, own, dm), BF16),
             pltpu.VMEM((n, own, dm), BF16),
             pltpu.VMEM((n, own, dm), BF16),
-            pltpu.VMEM((own, dm), BF16),
-            pltpu.VMEM((own, dm), BF16),
             pltpu.VMEM((2, 2, own, half), BF16),
             pltpu.VMEM((2, 2, own, half), BF16),
             pltpu.VMEM((2, 2, 2, own, half), BF16),
@@ -350,7 +373,7 @@
             pltpu.VMEM((ff, dm), F32),
             pltpu.SemaphoreType.DMA((N_MESSAGES,)),
             pltpu.SemaphoreType.DMA((N_MESSAGES,)),
-            pltpu.SemaphoreType.DMA((16,)),
+            pltpu.SemaphoreType.DMA((24,)),
         ],
         compiler_params=pltpu.CompilerParams(
             collective_id=0, has_side_effects=True, vmem_limit_bytes=63 * 1024 * 1024
@@ -360,10 +383,70 @@
     )(tokens, weight_in, bias_hidden, weight_out, out_grad)
 
 
+def settle_kernel(strip, *refs):
+    sources, (gw_in, gw_out, bias_o), stops, (in_sem, out_sem) = refs[:7], refs[7:10], refs[10:17], refs[17:]
+    sum_in, sum_out, bias, act, og, tok, pg = stops
+    started = []
+
+    def fetch(i, here=None):
+        src, dst = (sources[i], stops[i]) if here is None else (sources[i].at[here], stops[i].at[here])
+        copy = pltpu.make_async_copy(src, dst, in_sem.at[len(started)])
+        copy.start()
+        started.append(copy)
+        return copy
+
+    small = [fetch(i) for i in (3, 4)]
+    plan = [(1, sum_out, act, og, gw_out, at) for at in range(0, sum_out.shape[0], strip)]
+    fetched = [fetch(i, pl.ds(at, strip)) for i, *_, at in plan]
+    more = [fetch(i) for i in (5, 6, 2)]
+    plan_in = [(0, sum_in, tok, pg, gw_in, at) for at in range(0, sum_in.shape[0], strip)]
+    fetched += [fetch(i, pl.ds(at, strip)) for i, *_, at in plan_in]
+    onward = []
+
+    def give(src, dst):
+        copy = pltpu.make_async_copy(src, dst, out_sem.at[len(onward)])
+        copy.start()
+        onward.append(copy)
+
+    for copy in small:
+        copy.wait()
+    for step, (_, total, left, right, target, at) in enumerate(plan + plan_in):
+        if step == len(plan):
+            for copy in more:
+                copy.wait()
+            give(bias, bias_o)
+        fetched[step].wait()
+        turned = left[:, at : at + strip].T
+        for to, size in tiles(right.shape[1], 256):
+            total[at : at + strip, to : to + size] += dot_nn(turned, right[:, to : to + size])
+        give(total.at[pl.ds(at, strip)], target.at[pl.ds(at, strip)])
+    for copy in onward:
+        copy.wait()
+
+
+def settle(*parts):
+    any_space = pl.BlockSpec(memory_space=pl.ANY)
+    results = parts[:3]
+    strip = STRIP
+    n = sum(array.shape[0] // strip for array in results[:2]) + 5
+    return pl.pallas_call(
+        functools.partial(settle_kernel, strip),
+        out_shape=tuple(jax.ShapeDtypeStruct(array.shape, array.dtype) for array in results),
+        in_specs=[any_space] * len(parts),
+        out_specs=(any_space,) * len(results),
+        scratch_shapes=[pltpu.VMEM(array.shape, array.dtype) for array in parts]
+        + [pltpu.SemaphoreType.DMA((n,))] * 2,
+        compiler_params=pltpu.CompilerParams(vmem_limit_bytes=60 * 1024 * 1024),
+        cost_estimate=pl.CostEstimate(flops=2_400_000_000, bytes_accessed=28_000_000, transcendentals=0),
+        name="settle",
+    )(*parts)
+
+
 def local(tokens, weight_in, bias_hidden, weight_out, out_grad):
-    grad_tokens, grad_weight_in, grad_weight_out, grad_bias = exchange(
-        tokens, weight_in, bias_hidden, weight_out, out_grad
-    )
+    near_sum, for_pair, *rest = exchange(tokens, weight_in, bias_hidden, weight_out, out_grad)
+    from_pair = lax.ppermute(for_pair, "col", [(c, c ^ 2) for c in range(16)])
+    grad_weight_in, grad_weight_out, grad_bias = settle(*rest)
+    grad_tokens = (near_sum + from_pair.astype(F32)).astype(BF16)
     return (grad_tokens, grad_weight_in, grad_bias, grad_weight_out)
 
 

time: 147 us -> 139 us (0.946); the launches traced: 145 us -> 139 us
  local copies, waits for them, and re-layouts: 11.4 us -> 0.01 us
  Pallas kernels: 133 us -> 136 us
  starting transfers between devices: 0 us -> 1.6 us
    pallas_call x0 -> x1, Pallas kernels: none -> 12.3 us  [settle(): pl.pallas_call(functools.partial(settle_kernel, strip), out_shape=tuple((...]
    unnamed x10 -> x2, local copies, waits for them, and re-layouts: 11.4 us -> 0.01 us
    pallas_call x1, Pallas kernels: 133 us -> 123 us  [exchange(): pl.pallas_call(exchange_kernel, out_shape=(jax.ShapeDtypeStruct((own, dm)...]
    ppermute x0 -> x1, starting transfers between devices: none -> 1.6 us  [local(): from_pair = lax.ppermute(for_pair, 'col', [(c, c ^ 2) for c in range(16)])]
  transfers between devices with their start and end apart: 0 -> 1, of which waited for: 0 -> 0; matrix products, arithmetic and copies ran while one was open for 0% -> 0% of each run, Pallas kernels for 0% -> 9%
where the time goes in v3:
time: 139 us
  Pallas kernels  136 us (98%)
  starting transfers between devices  1.6 us (1%)
    pallas_call x1, Pallas kernels, exchange(): pl.pallas_call(exchange_kernel, out_shape=(jax.ShapeDtypeStruct((own, dm)...  123 us
    pallas_call x1, Pallas kernels, settle(): pl.pallas_call(functools.partial(settle_kernel, strip), out_shape=tuple((...  12.3 us
  transfers between devices with their start and end apart: 1, of which 0 were waited for; matrix products, arithmetic and copies ran while one was open for 0% of the time, Pallas kernels for 9%

profile of v3, /device:TPU:1, one launch (start us, length us, event | category | flops | bytes accessed | tf_op | source)
XLA Modules:
  0.0 138.6 jit_solution(16958407800865689517)
XLA Ops:
  0.6 123.2 %exchange.1 = (f32[96,1792]{1,0:T(8,128)}, bf16[96,1792]{1,0:T(8,128)(2,1)}, f32[1792,896]{1,0:T(8,128)}, f32[896,1792]{1,0:T(8,128)}, f32[896]{0:T(1024)}, /*in...) custom-call(bf16[96,1792]{1,0:T(8,128)(2,1)} %tok_h.1, ...), custom_call_target="tpu_custom_call" | custom-call | flops 24662507520 | bytes 40000000 | tf_op jit(solution)/shard_map/exchange/pallas_call | solution.py:337
  123.9 1.6 %collective-permute-start = (bf16[96,1792]{1,0:T(8,128)(2,1)}, bf16[96,1792]{1,0:T(8,128)(2,1)S(1)}, u32[]{:S(2)}, u32[]{:S(2)}) collective-permute-start(bf16[96,1792]{1,0:T(8,128)(2,1)} %get-tuple-element.17), channel_id=1, source_target_pairs={{0,2},{1,3},{2,0},{3,1},{4,6},{5,7},{6,4},{7,5},{8,10},{9,11},{10,... | collective-permute-start | bytes 1032200 | tf_op jit(solution)/shard_map/ppermute | solution.py:447
  125.5 0.0 copy-start
  125.5 12.3 %settle.1 = (f32[1792,896]{1,0:T(8,128)}, f32[896,1792]{1,0:T(8,128)}, f32[896]{0:T(1024)}) custom-call(f32[1792,896]{1,0:T(8,128)} %get-tuple-element.18.refs_0_, f32[896,1792]{1,0:T(8,128)} %get-tuple-element.19.refs_1_, f32[896]{0:T(1024)} %get-tuple-element.20.refs_2_, bf16[384,896]{1,0:T(8,128)(2,1)} %get-tuple-element.21.refs_3_, ...), custom_call_target="tpu_custom_call" | custom-call | flops 2400000000 | bytes 28000000 | tf_op jit(solution)/shard_map/settle/pallas_call | solution.py:432
  137.8 0.0 collective-permute-done
  137.8 0.0 copy-done
  137.8 0.8 add_convert_fusion
Async XLA Ops:
  123.9 13.9 %collective-permute-start = (bf16[96,1792]{1,0:T(8,128)(2,1)}, bf16[96,1792]{1,0:T(8,128)(2,1)S(1)}, u32[]{:S(2)}, u32[]{:S(2)}) collective-permute-start(bf16[96,1792]{1,0:T(8,128)(2,1)} %get-tuple-element.17), channel_id=1, source_target_pairs={{0,2},{1,3},{2,0},{3,1},{4,6},{5,7},{6,4},{7,5},{8,10},{9,11},{10,... | collective-permute-start | bytes 1032200 | tf_op jit(solution)/shard_map/ppermute | solution.py:447
  125.5 12.3 %copy-start = (f32[96,1792]{1,0:T(8,128)S(1)}, f32[96,1792]{1,0:T(8,128)}, u32[]{:S(2)}) copy-start(f32[96,1792]{1,0:T(8,128)} %get-tuple-element.16) | copy-start | bytes 2064388

commit v4 on v3

--- a/solution.py
+++ b/solution.py
@@ -13,34 +13,33 @@
 BF16 = jnp.bfloat16
 F32 = jnp.float32
 
-CHUNKS = ((0, 0), (3, 0), (1, 0), (1, 1), (2, 0), (2, 1), (3, 1), (0, 1))
+CHUNKS = ((0, 0), (3, 0), (2, 0), (1, 0), (1, 1), (2, 1), (0, 1), (3, 1))
 SCHEDULE = (
-    ("start",), ("load",), ("pre", 0), ("actp", 0), ("combp", 0), ("comba", 0), ("rel", 0, 1), ("rel", 0, 2),
-    ("rel", 0, 7), ("pre", 1), ("red", 0), ("combp", 1), ("pre", 2), ("rel", 1, 1), ("rel", 1, 2), ("rel", 1, 7),
-    ("actp", 1), ("act", 0), ("actp", 2), ("combp", 2), ("rel", 0, 4), ("rel", 0, 3), ("comba", 1), ("sprp", 0),
-    ("pre", 3), ("spra", 0), ("comba", 2), ("red", 1), ("rel", 1, 4), ("rel", 0, 6), ("grad", 0), ("combp", 3),
-    ("pre", 4), ("actp", 4), ("store", 0), ("join", 0), ("red", 2), ("gb", 0), ("act", 1), ("rel", 1, 6),
-    ("rel", 1, 3), ("combp", 4), ("comba", 4), ("actp", 3), ("sprp", 1), ("act", 2), ("spra", 1), ("rel", 0, 5),
-    ("red", 4), ("comba", 3), ("pre", 5), ("rel", 1, 5), ("grad", 1), ("gb", 1), ("actp", 5), ("spra", 2),
-    ("sprp", 2), ("join", 1), ("near0", 1, 0), ("act", 4), ("store", 1), ("red", 3), ("combp", 5), ("pre", 6),
-    ("actp", 6), ("comba", 5), ("store", 2), ("grad", 2), ("act", 3), ("gb", 2), ("sprp", 4), ("spra", 4),
-    ("join", 2), ("near0", 0, 0), ("combp", 6), ("pre", 7), ("comba", 6), ("actp", 7), ("red", 5), ("sprp", 3),
-    ("spra", 3), ("store", 4), ("grad", 4), ("act", 5), ("gb", 4), ("combp", 7), ("join", 4), ("red", 6),
-    ("comba", 7), ("store", 3), ("go", 0, 3), ("grad", 3), ("go", 1, 3), ("sprp", 5), ("near1", 0, 0), ("act", 6),
-    ("spra", 5), ("near1", 1, 0), ("join", 3), ("near0", 0, 1), ("go", 2, 3), ("red", 7), ("gi", 0, 3),
-    ("gi", 1, 3), ("grad", 5), ("spra", 6), ("sprp", 6), ("gi", 2, 3), ("fin",), ("gi", 3, 3), ("store", 5),
-    ("join", 5), ("act", 7), ("grad", 6), ("store", 6), ("gb", 3), ("go", 0, 5), ("go", 1, 5), ("join", 6),
-    ("near0", 1, 1), ("sprp", 7), ("go", 2, 5), ("gi", 0, 5), ("spra", 7), ("near1", 0, 1), ("near1", 1, 1),
-    ("gi", 1, 5), ("gi", 2, 5), ("grad", 7), ("gi", 3, 5), ("store", 7), ("gb", 5), ("gb", 6), ("gb", 7),
-    ("join", 7), ("xred1",),
+    ("start",), ("load",), ("pre", 0), ("actp", 0), ("combp", 0), ("comba", 0), ("rel", 0, 1), ("rel", 0, 3),
+    ("rel", 0, 6), ("pre", 1), ("red", 0), ("pre", 3), ("combp", 1), ("rel", 1, 6), ("rel", 1, 1), ("rel", 1, 3),
+    ("combp", 3), ("actp", 1), ("act", 0), ("actp", 3), ("rel", 0, 2), ("rel", 0, 4), ("comba", 1), ("sprp", 0),
+    ("pre", 2), ("pre", 4), ("spra", 0), ("comba", 3), ("red", 1), ("rel", 1, 4), ("rel", 0, 7), ("combp", 2),
+    ("grad", 0), ("actp", 4), ("combp", 4), ("store", 0), ("gb", 0), ("join", 0), ("act", 1), ("red", 3),
+    ("rel", 1, 7), ("rel", 1, 2), ("comba", 4), ("actp", 2), ("sprp", 1), ("spra", 1), ("act", 3), ("red", 4),
+    ("rel", 0, 5), ("rel", 1, 5), ("comba", 2), ("store", 1), ("pre", 5), ("grad", 1), ("actp", 5), ("sprp", 3),
+    ("pre", 7), ("spra", 3), ("act", 4), ("join", 1), ("combp", 5), ("near0", 1, 0), ("actp", 7), ("red", 2),
+    ("gb", 1), ("combp", 7), ("comba", 5), ("store", 3), ("grad", 3), ("gb", 3), ("act", 2), ("spra", 4),
+    ("join", 3), ("near0", 0, 0), ("sprp", 4), ("comba", 7), ("red", 5), ("sprp", 2), ("pre", 6), ("spra", 2),
+    ("actp", 6), ("store", 4), ("grad", 4), ("act", 5), ("combp", 6), ("red", 7), ("gb", 4), ("join", 4),
+    ("near0", 0, 1), ("store", 2), ("grad", 2), ("gb", 2), ("go", 0, 3), ("go", 1, 3), ("comba", 6), ("join", 2),
+    ("go", 2, 3), ("spra", 5), ("sprp", 5), ("act", 7), ("gi", 0, 3), ("gi", 1, 3), ("gi", 2, 3), ("red", 6),
+    ("store", 5), ("gi", 3, 3), ("grad", 5), ("near1", 0, 0), ("near1", 1, 0), ("go", 0, 5), ("spra", 7),
+    ("sprp", 7), ("go", 1, 5), ("join", 5), ("go", 2, 5), ("gi", 0, 5), ("act", 6), ("grad", 7), ("fin",),
+    ("store", 7), ("gi", 1, 5), ("gi", 2, 5), ("join", 7), ("near0", 1, 1), ("sprp", 6), ("gi", 3, 5),
+    ("near1", 0, 1), ("near1", 1, 1), ("gb", 5), ("spra", 6), ("gb", 7), ("grad", 6), ("gb", 6), ("store", 6),
+    ("join", 6), ("xred1",),
 )
 SLOT = {where: at for at, where in enumerate(CHUNKS)}
 N_CHUNKS = len(CHUNKS)
 GROUPS = {3: (0, 4), 5: (4, 6)}
 LATE = 6
-STRIP = 128
-OUT_STRIPS = ((0, 2), (2, 4), (4, 7))
-IN_STRIPS = ((0, 3), (3, 7), (7, 10), (10, 14))
+OUT_STRIP, OUT_STRIPS = 128, ((0, 2), (2, 4), (4, 7))
+IN_STRIP, IN_STRIPS = 256, ((0, 2), (2, 4), (4, 6), (6, 7))
 N_MESSAGES = 192
 
 
@@ -235,15 +234,15 @@
 
     started, done = set(), {"in": 0, "out": 0, "bias": 0}
 
-    def accumulate(acc, left, right, k, strips):
+    def accumulate(acc, left, right, k, strip, strips):
         first = (id(acc), strips) not in started
         started.add((id(acc), strips))
         group = pl.ds(GROUPS[k][0], GROUPS[k][1] - GROUPS[k][0])
         depth = (GROUPS[k][1] - GROUPS[k][0]) * 2 * own
 
         def body(i, carry):
-            at = pl.ds(pl.multiple_of(i * STRIP, STRIP), STRIP)
-            turned = left[group, :, at].reshape(depth, STRIP).T
+            at = pl.ds(pl.multiple_of(i * strip, strip), strip)
+            turned = left[group, :, at].reshape(depth, strip).T
             for to, size in tiles(right.shape[-1], 256):
                 product = dot_nn(turned, right[group, :, to : to + size].reshape(depth, size))
                 acc[at, to : to + size] = product if first else acc[at, to : to + size] + product
@@ -252,13 +251,13 @@
         lax.fori_loop(*strips, body, 0)
 
     def weight_out_part(at, k):
-        accumulate(acc_out, act, og, k, OUT_STRIPS[at])
+        accumulate(acc_out, act, og, k, OUT_STRIP, OUT_STRIPS[at])
         done["out"] += 1
         if done["out"] == len(GROUPS) * len(OUT_STRIPS):
             local_copy(acc_out, gw_out)
 
     def weight_in_part(at, k):
-        accumulate(acc_in, tok, pg, k, IN_STRIPS[at])
+        accumulate(acc_in, tok, pg, k, IN_STRIP, IN_STRIPS[at])
         done["in"] += 1
         if done["in"] == len(GROUPS) * len(IN_STRIPS):
             local_copy(acc_in, gw_in)
@@ -396,11 +395,11 @@
         return copy
 
     small = [fetch(i) for i in (3, 4)]
-    plan = [(1, sum_out, act, og, gw_out, at) for at in range(0, sum_out.shape[0], strip)]
-    fetched = [fetch(i, pl.ds(at, strip)) for i, *_, at in plan]
+    plan = [(1, sum_out, act, og, gw_out, at) for at in tiles(sum_out.shape[0], strip)]
+    fetched = [fetch(i, pl.ds(*at)) for i, *_, at in plan]
     more = [fetch(i) for i in (5, 6, 2)]
-    plan_in = [(0, sum_in, tok, pg, gw_in, at) for at in range(0, sum_in.shape[0], strip)]
-    fetched += [fetch(i, pl.ds(at, strip)) for i, *_, at in plan_in]
+    plan_in = [(0, sum_in, tok, pg, gw_in, at) for at in tiles(sum_in.shape[0], strip)]
+    fetched += [fetch(i, pl.ds(*at)) for i, *_, at in plan_in]
     onward = []
 
     def give(src, dst):
@@ -410,16 +409,16 @@
 
     for copy in small:
         copy.wait()
-    for step, (_, total, left, right, target, at) in enumerate(plan + plan_in):
+    for step, (_, total, left, right, target, (at, rows)) in enumerate(plan + plan_in):
         if step == len(plan):
             for copy in more:
                 copy.wait()
             give(bias, bias_o)
         fetched[step].wait()
-        turned = left[:, at : at + strip].T
+        turned = left[:, at : at + rows].T
         for to, size in tiles(right.shape[1], 256):
-            total[at : at + strip, to : to + size] += dot_nn(turned, right[:, to : to + size])
-        give(total.at[pl.ds(at, strip)], target.at[pl.ds(at, strip)])
+            total[at : at + rows, to : to + size] += dot_nn(turned, right[:, to : to + size])
+        give(total.at[pl.ds(at, rows)], target.at[pl.ds(at, rows)])
     for copy in onward:
         copy.wait()
 
@@ -427,8 +426,8 @@
 def settle(*parts):
     any_space = pl.BlockSpec(memory_space=pl.ANY)
     results = parts[:3]
-    strip = STRIP
-    n = sum(array.shape[0] // strip for array in results[:2]) + 5
+    strip = 256
+    n = sum(len(tiles(array.shape[0], strip)) for array in results[:2]) + 5
     return pl.pallas_call(
         functools.partial(settle_kernel, strip),
         out_shape=tuple(jax.ShapeDtypeStruct(array.shape, array.dtype) for array in results),

time: 139 us -> 136 us (0.978)
  Pallas kernels: 136 us -> 132 us
    pallas_call x1, Pallas kernels: 123 us -> 122 us  [exchange(): pl.pallas_call(exchange_kernel, out_shape=(jax.ShapeDtypeStruct((own, dm)...]
  transfers between devices with their start and end apart: 1 -> 1, of which waited for: 0 -> 0; matrix products, arithmetic and copies ran while one was open for 0% -> 0% of each run, Pallas kernels for 9% -> 8%
where the time goes in v4:
time: 136 us; the launch traced here: 135 us
  Pallas kernels  132 us (97%)
    pallas_call x1, Pallas kernels, exchange(): pl.pallas_call(exchange_kernel, out_shape=(jax.ShapeDtypeStruct((own, dm)...  122 us
    pallas_call x1, Pallas kernels, settle(): pl.pallas_call(functools.partial(settle_kernel, strip), out_shape=tuple((...  10.9 us
  transfers between devices with their start and end apart: 1, of which 0 were waited for; matrix products, arithmetic and copies ran while one was open for 0% of the time, Pallas kernels for 8%

profile of v4, /device:TPU:1, one launch (start us, length us, event | category | flops | bytes accessed | tf_op | source)
XLA Modules:
  0.0 134.7 jit_solution(2034450014451976474)
XLA Ops:
  0.6 121.5 %exchange.1 = (f32[96,1792]{1,0:T(8,128)}, bf16[96,1792]{1,0:T(8,128)(2,1)}, f32[1792,896]{1,0:T(8,128)}, f32[896,1792]{1,0:T(8,128)}, f32[896]{0:T(1024)}, /*in...) custom-call(bf16[96,1792]{1,0:T(8,128)(2,1)} %tok_h.1, ...), custom_call_target="tpu_custom_call" | custom-call | flops 24662507520 | bytes 40000000 | tf_op jit(solution)/shard_map/exchange/pallas_call | solution.py:336
  122.2 0.8 collective-permute-start
  123.0 0.0 copy-start
  123.0 10.9 %settle.1 = (f32[1792,896]{1,0:T(8,128)}, f32[896,1792]{1,0:T(8,128)}, f32[896]{0:T(1024)}) custom-call(f32[1792,896]{1,0:T(8,128)} %get-tuple-element.18.refs_0_, f32[896,1792]{1,0:T(8,128)} %get-tuple-element.19.refs_1_, f32[896]{0:T(1024)} %get-tuple-element.20.refs_2_, bf16[384,896]{1,0:T(8,128)(2,1)} %get-tuple-element.21.refs_3_, ...), custom_call_target="tpu_custom_call" | custom-call | flops 2400000000 | bytes 28000000 | tf_op jit(solution)/shard_map/settle/pallas_call | solution.py:431
  133.9 0.0 collective-permute-done
  133.9 0.0 copy-done
  133.9 0.8 add_convert_fusion
Async XLA Ops:
  122.2 11.8 %collective-permute-start = (bf16[96,1792]{1,0:T(8,128)(2,1)}, bf16[96,1792]{1,0:T(8,128)(2,1)S(1)}, u32[]{:S(2)}, u32[]{:S(2)}) collective-permute-start(bf16[96,1792]{1,0:T(8,128)(2,1)} %get-tuple-element.17), channel_id=1, source_target_pairs={{0,2},{1,3},{2,0},{3,1},{4,6},{5,7},{6,4},{7,5},{8,10},{9,11},{10,... | collective-permute-start | bytes 1032200 | tf_op jit(solution)/shard_map/ppermute | solution.py:446
  123.0 10.9 %copy-start = (f32[96,1792]{1,0:T(8,128)S(1)}, f32[96,1792]{1,0:T(8,128)}, u32[]{:S(2)}) copy-start(f32[96,1792]{1,0:T(8,128)} %get-tuple-element.16) | copy-start | bytes 2064388

commit v5 on v4

--- a/solution.py
+++ b/solution.py
@@ -38,7 +38,7 @@
 N_CHUNKS = len(CHUNKS)
 GROUPS = {3: (0, 4), 5: (4, 6)}
 LATE = 6
-OUT_STRIP, OUT_STRIPS = 128, ((0, 2), (2, 4), (4, 7))
+OUT_STRIPS = (((256, (0, 1)),), ((256, (1, 2)),), ((256, (2, 3)), (128, (6, 7))))
 IN_STRIP, IN_STRIPS = 256, ((0, 2), (2, 4), (4, 6), (6, 7))
 N_MESSAGES = 192
 
@@ -251,7 +251,8 @@
         lax.fori_loop(*strips, body, 0)
 
     def weight_out_part(at, k):
-        accumulate(acc_out, act, og, k, OUT_STRIP, OUT_STRIPS[at])
+        for strip, strips in OUT_STRIPS[at]:
+            accumulate(acc_out, act, og, k, strip, strips)
         done["out"] += 1
         if done["out"] == len(GROUPS) * len(OUT_STRIPS):
             local_copy(acc_out, gw_out)

time: 136 us -> 135 us (level)
  no operation moved by 1% of the time
where the time goes in v5:
time: 135 us; the launch traced here: 134 us
  Pallas kernels  132 us (98%)
    pallas_call x1, Pallas kernels, exchange(): pl.pallas_call(exchange_kernel, out_shape=(jax.ShapeDtypeStruct((own, dm)...  121 us
    pallas_call x1, Pallas kernels, settle(): pl.pallas_call(functools.partial(settle_kernel, strip), out_shape=tuple((...  10.9 us
  transfers between devices with their start and end apart: 1, of which 0 were waited for; matrix products, arithmetic and copies ran while one was open for 0% of the time, Pallas kernels for 8%

profile of v5, /device:TPU:1, one launch (start us, length us, event | category | flops | bytes accessed | tf_op | source)
XLA Modules:
  0.0 134.1 jit_solution(17908512977557343848)
XLA Ops:
  0.6 121.2 %exchange.1 = (f32[96,1792]{1,0:T(8,128)}, bf16[96,1792]{1,0:T(8,128)(2,1)}, f32[1792,896]{1,0:T(8,128)}, f32[896,1792]{1,0:T(8,128)}, f32[896]{0:T(1024)}, /*in...) custom-call(bf16[96,1792]{1,0:T(8,128)(2,1)} %tok_h.1, ...), custom_call_target="tpu_custom_call" | custom-call | flops 24662507520 | bytes 40000000 | tf_op jit(solution)/shard_map/exchange/pallas_call | solution.py:337
  121.8 0.6 collective-permute-start
  122.4 0.0 copy-start
  122.4 10.9 %settle.1 = (f32[1792,896]{1,0:T(8,128)}, f32[896,1792]{1,0:T(8,128)}, f32[896]{0:T(1024)}) custom-call(f32[1792,896]{1,0:T(8,128)} %get-tuple-element.18.refs_0_, f32[896,1792]{1,0:T(8,128)} %get-tuple-element.19.refs_1_, f32[896]{0:T(1024)} %get-tuple-element.20.refs_2_, bf16[384,896]{1,0:T(8,128)(2,1)} %get-tuple-element.21.refs_3_, ...), custom_call_target="tpu_custom_call" | custom-call | flops 2400000000 | bytes 28000000 | tf_op jit(solution)/shard_map/settle/pallas_call | solution.py:432
  133.3 0.0 collective-permute-done
  133.3 0.0 copy-done
  133.3 0.8 add_convert_fusion
Async XLA Ops:
  121.8 11.5 %collective-permute-start = (bf16[96,1792]{1,0:T(8,128)(2,1)}, bf16[96,1792]{1,0:T(8,128)(2,1)S(1)}, u32[]{:S(2)}, u32[]{:S(2)}) collective-permute-start(bf16[96,1792]{1,0:T(8,128)(2,1)} %get-tuple-element.17), channel_id=1, source_target_pairs={{0,2},{1,3},{2,0},{3,1},{4,6},{5,7},{6,4},{7,5},{8,10},{9,11},{10,... | collective-permute-start | bytes 1032200 | tf_op jit(solution)/shard_map/ppermute | solution.py:447
  122.4 11.0 %copy-start = (f32[96,1792]{1,0:T(8,128)S(1)}, f32[96,1792]{1,0:T(8,128)}, u32[]{:S(2)}) copy-start(f32[96,1792]{1,0:T(8,128)} %get-tuple-element.16) | copy-start | bytes 2064388
